TPU v7x, 128 devices: a whole 4x4x4 slice. The times are simulated.
128 devices in a mesh: gx: 32 (over z, x, y_hi), gy: 4 (over y_lo, core).
Axes of the slice: x: 4, y: 4 (y_hi: 2, y_lo: 2; y = y_hi * 2 + y_lo), z: 4, core: 2. Of those that a mesh axis runs over, the one named last changes fastest.
Arguments:
- rhs_field: float32 [2, 8, 256, 1024], P(None, None, 'gx', 'gy'), may hold values from -6 to 6
- permittivity: float32 [8, 256, 1024], P(None, 'gx', 'gy'), may hold values from 1 to 4
- surf_dist: float32 [16384, 128], P(('gx', 'gy')), may hold values from 0.2 to 1
- surf_normal: float32 [3, 16384, 128], P(None, ('gx', 'gy')), may hold values from -4 to 4
- surf_inc: float32 [2, 16384, 128], P(None, ('gx', 'gy')), may hold values from -6 to 6
- surf_cell: int32 [16384, 128], P(('gx', 'gy')), may hold values from 0 to 16383
- surf_mask: int32 [16384, 128], P(('gx', 'gy')), may hold values 0 or 1
- surf_owner: int32 [16384, 1], P(('gx', 'gy')), may hold values from 0 to 127; in each aligned block of 128 rows (0 to 127, 128 to 255, ...) at most 2 rows name the same one
Outputs:
- solution: float32 [2, 8, 256, 1024], P(None, None, 'gx', 'gy')
- residual: float32 [2, 8, 256, 1024], P(None, None, 'gx', 'gy')
Inputs may be any that keep to these rules, and one draw needn't show every extreme that they name: `surf_owner`: within the 128 rows of one device no owner is named more than 2 times, a bound that some block reaches.
All inputs are finite; a program needn't handle non-finite values. No bound on the sum of `surf_mask` on one device may be relied on, other than what follows from the above.
Results may differ from a plain program's by a relative error of at most 0.00002.
Values sent between devices are 32-bit elements; how exact they have to be, the bound alone decides.
No kernel may reach another device: no remote copies, remote signals or barrier semaphores. Data moves between devices by JAX's collectives and lax.ppermute only.
A program may use at most 128 MiB of HBM per device.

v0:
```python
import functools

import jax
import jax.numpy as jnp
from jax import lax
from jax.experimental import pallas as pl
from jax.experimental.pallas import tpu as pltpu
from jax.sharding import PartitionSpec as P

CAP = 2
K_SQUARED = 0.25
BETA = 0.5
OMEGA = 0.8
TAU = 1.0

CHANNELS = 6
GROUP = 128

f32 = jnp.float32
bf16 = jnp.bfloat16


def pack_kernel(
    owner_hbm, dist_hbm, normal_hbm, inc_hbm, cell_hbm, mask_hbm, out_ref,
    owner_ref, base_ref, count_ref, dist_ref, coef_ref, cell_ref, mask_ref, sems,
):
    blocks = dist_ref.shape[0]
    devices = count_ref.shape[0]
    copies = [
        pltpu.make_async_copy(owner_hbm, owner_ref, sems.at[0]),
        pltpu.make_async_copy(dist_hbm, dist_ref, sems.at[1]),
        pltpu.make_async_copy(normal_hbm, coef_ref.at[pl.ds(0, 3)], sems.at[2]),
        pltpu.make_async_copy(inc_hbm, coef_ref.at[pl.ds(3, 2)], sems.at[3]),
        pltpu.make_async_copy(cell_hbm, cell_ref, sems.at[4]),
        pltpu.make_async_copy(mask_hbm, mask_ref, sems.at[5]),
    ]
    for copy in copies:
        copy.start()
    out_ref[...] = jnp.full(out_ref.shape, -1.0, f32)

    def clear(i, carry):
        count_ref[i] = 0
        return carry

    lax.fori_loop(0, devices, clear, 0, unroll=8)
    copies[0].wait()

    def rank(b, carry):
        owner = owner_ref[b]
        seen = count_ref[owner]
        count_ref[owner] = seen + 1
        base_ref[b] = (owner * CAP + seen) * CHANNELS
        return carry

    lax.fori_loop(0, blocks, rank, 0, unroll=8)
    for copy in copies[1:]:
        copy.wait()
    half = 0.5 * TAU * dist_ref[...]
    for k in range(3):
        coef_ref[k] = half * coef_ref[k]
    for k in range(3, 5):
        coef_ref[k] = TAU * coef_ref[k]
    coef_ref[5] = jnp.where(mask_ref[...] > 0, cell_ref[...], 1 << 14).astype(f32)

    def place(b, carry):
        base = base_ref[b]
        for c in range(CHANNELS):
            out_ref[pl.ds(base + c, 1), :] = coef_ref[c, pl.ds(b, 1), :]
        return carry

    lax.fori_loop(0, blocks, place, 0, unroll=8)


def scatter_slots(recv_ref, hi_ref, lo_ref, acc_ref, channels, count):
    slots = hi_ref.shape[0]
    lo_n = acc_ref.shape[1]
    hi_n = acc_ref.shape[0] // (2 * len(channels) + count)
    group = min(GROUP, slots)
    chunk = min(64, slots)
    for i in range(0, slots, chunk):
        cell = recv_ref[pl.ds(i * CHANNELS + CHANNELS - 1, chunk, stride=CHANNELS), :].astype(jnp.int32)
        hi_ref[i : i + chunk] = (cell >> 8).astype(f32)
        lo_ref[i : i + chunk] = (cell & 255).astype(f32)
    acc_ref[...] = jnp.zeros(acc_ref.shape, f32)
    hi_iota = lax.broadcasted_iota(jnp.int32, (hi_n, 128), 0).astype(f32).astype(bf16)
    lo_iota = lax.broadcasted_iota(jnp.int32, (lo_n, 128), 0).astype(f32).astype(bf16)
    one = jnp.ones((), bf16)
    zero = jnp.zeros((), bf16)

    def row(ref, index):
        return jnp.broadcast_to(ref[pl.ds(index, 1), :], (16, 128))

    def tall(tile, n):
        return jnp.concatenate([tile] * (n // 16), axis=0)

    def step(g, carry):
        left, right = [], []
        for j in range(group):
            slot = g * group + j
            hot = hi_iota == tall(row(hi_ref, slot).astype(bf16), hi_n)
            pieces = []
            for c in channels:
                value = row(recv_ref, slot * CHANNELS + c)
                lead = value.astype(bf16)
                rest = (value - lead.astype(f32)).astype(bf16)
                pieces.append(jnp.where(hot, tall(lead, hi_n), zero))
                pieces.append(jnp.where(hot, tall(rest, hi_n), zero))
            if count:
                pieces.append(jnp.where(hot, one, zero))
            left.append(jnp.concatenate(pieces, axis=0))
            right.append(jnp.where(lo_iota == tall(row(lo_ref, slot).astype(bf16), lo_n), one, zero))
        acc_ref[...] += lax.dot_general(
            jnp.concatenate(left, axis=1),
            jnp.concatenate(right, axis=1),
            (((1,), (1,)), ((), ())),
            preferred_element_type=f32,
        )
        return carry

    lax.fori_loop(0, slots // group, step, 0)

    def channel(k):
        return acc_ref[2 * k * hi_n : (2 * k + 1) * hi_n, :] + acc_ref[(2 * k + 1) * hi_n : (2 * k + 2) * hi_n, :]

    return [channel(k) for k in range(len(channels))] + ([acc_ref[2 * len(channels) * hi_n :, :]] if count else [])


def keep_tiles(ref, k, value):
    for t in range(ref.shape[1]):
        ref[k, t] = value[:, t * 128 : (t + 1) * 128]


def pack_rows(out_ref, item, ref, k, row, gate=None):
    planes = ref.shape[2] // 8
    for t in range(ref.shape[1]):
        value = ref[k, t, pl.ds(row, planes, stride=8), :]
        if gate is not None:
            value = jnp.where(gate, 0.0, value)
        out_ref[item * planes : (item + 1) * planes, t * 128 : (t + 1) * 128] = value


def unpack_rows(ref, k, row, in_ref, item):
    planes = ref.shape[2] // 8
    for t in range(ref.shape[1]):
        value = in_ref[item * planes : (item + 1) * planes, t * 128 : (t + 1) * 128]
        ref[k, t, pl.ds(row, planes, stride=8), :] = value


def incident_kernel(recv_ref, rhs_ref, perm_ref, r1_ref, up_ref, down_ref, hi_ref, lo_ref, acc_ref, tile_ref):
    parts = scatter_slots(recv_ref, hi_ref, lo_ref, acc_ref, (3, 4), 0)
    for k in range(2):
        value = rhs_ref[k] - parts[k]
        r1_ref[k] = value
        keep_tiles(tile_ref, k, value)
    keep_tiles(tile_ref, 2, perm_ref[...])
    place = lax.axis_index("gx")
    for out_ref, start, edge in ((up_ref, 0, 0), (down_ref, 5, lax.axis_size("gx") - 1)):
        for c in range(3):
            for k in range(3):
                pack_rows(out_ref, 3 * c + k, tile_ref, c, start + k, place == edge if c == 2 else None)


def coefficient_kernel(recv_ref, wn_ref, up_ref, down_ref, hi_ref, lo_ref, acc_ref, tile_ref):
    nz, nx, ny, w = scatter_slots(recv_ref, hi_ref, lo_ref, acc_ref, (0, 1, 2), 1)
    for k, value in enumerate((TAU * w, nz, nx, ny)):
        wn_ref[k] = value
        keep_tiles(tile_ref, k, value)
        pack_rows(up_ref, k, tile_ref, k, 0)
        pack_rows(down_ref, k, tile_ref, k, 7)


COL_PLACE = ((0, 3), (3, 3), (6, 3), (9, 1), (10, 1), (11, 1), (12, 1))


def strip_kernel(r1_ref, perm_ref, wn_ref, above_ref, below_ref, left_ref, right_ref, halo_ref):
    planes = perm_ref.shape[0] // 8
    lo_n = perm_ref.shape[1]
    halo_ref[...] = jnp.zeros(halo_ref.shape, f32)
    for c in range(3):
        for k in range(3):
            unpack_rows(halo_ref, c, k, below_ref, 3 * c + k)
            unpack_rows(halo_ref, c, 5 + k, above_ref, 3 * c + k)
    lane = lax.broadcasted_iota(jnp.int32, (planes, 16, 128), 2)
    position = lax.axis_index("gy")
    last = lax.axis_size("gy") - 1
    nothing = jnp.zeros((planes, 8, 128), f32)
    for out_ref, start, sign, edge in ((left_ref, 0, 1, 0), (right_ref, lo_n - 128, -1, last)):
        lanes = pl.ds(start, 128)
        place = lane if sign > 0 else 127 - lane
        strip = jnp.zeros((planes, 16, 128), f32)
        for c in range(7):
            if c < 3:
                own = perm_ref[:, lanes] if c == 2 else r1_ref[c, :, lanes]
                other = halo_ref[c, start // 128].reshape(planes, 8, 128)
            else:
                own, other = wn_ref[c - 3, :, lanes], nothing
            full = jnp.concatenate([own.reshape(planes, 8, 128), other], axis=1)
            offset, width = COL_PLACE[c]
            moved = pltpu.roll(full, (sign * offset) % 128, axis=2)
            strip = jnp.where((place >= offset) & (place < offset + width), moved, strip)
        out_ref[...] = jnp.where(position == edge, 0.0, strip)


def final_kernel(
    r1_ref, perm_ref, wn_ref, halo_ref, above_ref, below_ref, fleft_ref, fright_ref, sol_ref, res_ref, edge_ref
):
    planes = perm_ref.shape[0] // 8
    lo_n = perm_ref.shape[1]
    wide = lo_n + 128
    lane = lax.broadcasted_iota(jnp.int32, (planes, 16, 128), 2)
    edge_ref[...] = jnp.zeros(edge_ref.shape, f32)
    for k in range(4):
        unpack_rows(edge_ref, k, 0, below_ref, k)
        unpack_rows(edge_ref, k, 7, above_ref, k)

    def extended(c):
        if c < 3:
            own = perm_ref[...] if c == 2 else r1_ref[c]
            other = [halo_ref[c, t] for t in range(lo_n // 128)]
        else:
            own = wn_ref[c - 3]
            other = [edge_ref[c - 3, t] for t in range(lo_n // 128)]
        other = jnp.concatenate([t.reshape(planes, 8, 128) for t in other], axis=2)
        body = jnp.concatenate([own.reshape(planes, 8, lo_n), other], axis=1)
        offset, width = COL_PLACE[c]
        right = pltpu.roll(fright_ref[...], (-offset) % 128, axis=2)
        left = pltpu.roll(fleft_ref[...], offset, axis=2)
        side = jnp.where(lane < width, right, jnp.where(lane >= 128 - width, left, 0.0))
        return jnp.concatenate([body, side], axis=2)

    re, im, perm, w, nz, nx, ny = [extended(c) for c in range(7)]
    diag = 6.0 - K_SQUARED * perm
    shift = BETA * K_SQUARED * perm
    denom = diag * diag + shift * shift
    inside = perm > 0.5
    inv_re = jnp.where(inside, OMEGA * diag / denom, 0.0)
    inv_im = jnp.where(inside, -OMEGA * shift / denom, 0.0)

    def damp(a, b):
        return a * inv_re - b * inv_im, a * inv_im + b * inv_re

    def sides(v):
        nothing = jnp.zeros((1,) + v.shape[1:], f32)
        after = jnp.concatenate([v[1:], nothing], axis=0)
        before = jnp.concatenate([nothing, v[:-1]], axis=0)
        return (
            (after, before),
            (pltpu.roll(v, 15, axis=1), pltpu.roll(v, 1, axis=1)),
            (pltpu.roll(v, wide - 1, axis=2), pltpu.roll(v, 1, axis=2)),
        )

    def helm(v, pairs):
        total = pairs[0][0] + pairs[0][1]
        for a, b in pairs[1:]:
            total = total + a + b
        return diag * v - total

    def swept(a, b):
        za, zb = damp(a, b)
        ma = helm(za, sides(za)) - shift * zb
        mb = helm(zb, sides(zb)) + shift * za
        da, db = damp(a - ma, b - mb)
        return za + da, zb + db

    def surface(v, pairs):
        (a, b), (c, d), (e, f) = pairs
        return w * v + nz * (a - b) + nx * (c - d) + ny * (e - f)

    def remaining(r, v):
        pairs = sides(v)
        return r - helm(v, pairs) - surface(v, pairs)

    sa, sb = swept(re, im)
    ra, rb = remaining(re, sa), remaining(im, sb)
    ua, ub = swept(ra, rb)
    res_ref[0] = ra[:, 0:8, 0:lo_n]
    res_ref[1] = rb[:, 0:8, 0:lo_n]
    sol_ref[0] = (sa + ua)[:, 0:8, 0:lo_n]
    sol_ref[1] = (sb + ub)[:, 0:8, 0:lo_n]


def in_vmem(n):
    return [pl.BlockSpec(memory_space=pltpu.VMEM)] * n


def shape(*dims):
    return jax.ShapeDtypeStruct(dims, f32)


def per_device(rhs_field, permittivity, surf_dist, surf_normal, surf_inc, surf_cell, surf_mask, surf_owner):
    planes, rows, cols = permittivity.shape
    blocks, points = surf_cell.shape
    gx, gy = lax.axis_size("gx"), lax.axis_size("gy")
    devices = gx * gy
    slots = devices * CAP
    params = pltpu.CompilerParams(vmem_limit_bytes=48 << 20)
    send = pl.pallas_call(
        pack_kernel,
        out_shape=shape(slots * CHANNELS, points),
        in_specs=[pl.BlockSpec(memory_space=pltpu.HBM)] * 6,
        out_specs=pl.BlockSpec(memory_space=pltpu.VMEM),
        scratch_shapes=[
            pltpu.SMEM((blocks,), jnp.int32),
            pltpu.SMEM((blocks,), jnp.int32),
            pltpu.SMEM((devices,), jnp.int32),
            pltpu.VMEM((blocks, points), f32),
            pltpu.VMEM((CHANNELS, blocks, points), f32),
            pltpu.VMEM((blocks, points), jnp.int32),
            pltpu.VMEM((blocks, points), jnp.int32),
            pltpu.SemaphoreType.DMA((6,)),
        ],
        compiler_params=params,
        name="pack",
    )(*[
        pltpu.with_memory_space_constraint(x, pltpu.HBM)
        for x in (surf_owner[:, 0], surf_dist, surf_normal, surf_inc, surf_cell, surf_mask)
    ])
    recv = lax.all_to_all(send.reshape(-1), ("gx", "gy"), split_axis=0, concat_axis=0, tiled=True)
    recv = recv.reshape(slots * CHANNELS, points)
    cells = planes * rows
    rhs_field = rhs_field.reshape(2, cells, cols)
    permittivity = permittivity.reshape(cells, cols)

    def scatter_scratch(parts, kept):
        return [
            pltpu.VMEM((slots, points), f32),
            pltpu.VMEM((slots, points), f32),
            pltpu.VMEM((parts * cells, cols), f32),
            pltpu.VMEM((kept, cols // 128, cells, 128), f32),
        ]

    r1, up, down = pl.pallas_call(
        incident_kernel,
        out_shape=(shape(2, cells, cols), shape(9 * planes, cols), shape(9 * planes, cols)),
        in_specs=in_vmem(3),
        out_specs=tuple(in_vmem(3)),
        scratch_shapes=scatter_scratch(4, 3),
        compiler_params=params,
        name="incident",
    )(recv, rhs_field, permittivity)
    after_x = [(i, (i + 1) % gx) for i in range(gx)]
    before_x = [(j, i) for i, j in after_x]
    after_y = [(i, (i + 1) % gy) for i in range(gy)]
    before_y = [(j, i) for i, j in after_y]
    above = lax.ppermute(down, "gx", after_x)
    below = lax.ppermute(up, "gx", before_x)
    flops = 2 * 7 * cells * cols * slots * points
    wn, up, down = pl.pallas_call(
        coefficient_kernel,
        out_shape=(shape(4, cells, cols), shape(4 * planes, cols), shape(4 * planes, cols)),
        in_specs=in_vmem(1),
        out_specs=tuple(in_vmem(3)),
        scratch_shapes=scatter_scratch(7, 4),
        compiler_params=params,
        cost_estimate=pl.CostEstimate(flops=flops, transcendentals=0, bytes_accessed=slots * CHANNELS * points * 4),
        name="coefficient",
    )(recv)
    above_wn = lax.ppermute(down, "gx", after_x)
    below_wn = lax.ppermute(up, "gx", before_x)
    to_left, to_right, halo = pl.pallas_call(
        strip_kernel,
        out_shape=(shape(planes, 16, 128), shape(planes, 16, 128), shape(3, cols // 128, cells, 128)),
        in_specs=in_vmem(5),
        out_specs=tuple(in_vmem(3)),
        compiler_params=params,
        name="strips",
    )(r1, permittivity, wn, above, below)
    from_left = lax.ppermute(to_right, "gy", after_y)
    from_right = lax.ppermute(to_left, "gy", before_y)
    field = shape(2, planes, rows, cols)
    return pl.pallas_call(
        final_kernel,
        out_shape=(field, field),
        in_specs=in_vmem(8),
        out_specs=tuple(in_vmem(2)),
        scratch_shapes=[pltpu.VMEM((4, cols // 128, cells, 128), f32)],
        compiler_params=params,
        name="final",
    )(r1, permittivity, wn, halo, above_wn, below_wn, from_left, from_right)


def solution(mesh):
    split = ("gx", "gy")
    placed = (
        P(None, None, "gx", "gy"),
        P(None, "gx", "gy"),
        P(split, None),
        P(None, split, None),
        P(None, split, None),
        P(split, None),
        P(split, None),
        P(split, None),
    )
    return jax.shard_map(
        per_device,
        mesh=mesh,
        in_specs=placed,
        out_specs=(P(None, None, "gx", "gy"), P(None, None, "gx", "gy")),
        check_vma=False,
    )
```

profile of v0, /device:TPU:0, one launch (start us, length us, event | category | flops | bytes accessed | tf_op | source)
XLA Modules:
  0.0 63.9 jit_solution(17234129035609353638)
XLA Ops:
  0.6 1.7 %pack.1 = f32[1536,128]{1,0:T(8,128)S(1)} custom-call(s32[128]{0:T(128)} %bitcast.12, f32[128,128]{1,0:T(8,128)} %dist_hbm.1, f32[3,128,128]{2,1,0:T(8,128)} %normal_hbm.1, f32[2,128,128]{2,1,0:T(8,128)} %inc_hbm.1, s32[128,128]{1,0:T(8,128)} %cell_hbm.1, s32[128,128]{1,0:T(8,128)} %mask_hbm.1), custom_call_target="tpu_custom_call" | custom-call | tf_op jit(solution)/shard_map/pack/pallas_call | solution.py:297
  2.3 0.0 copy-start
  2.4 0.0 copy-start.1
  2.4 27.2 %all_to_all.9 = f32[128,1536,1]{1,2,0:T(1,128)S(1)} all-to-all(f32[128,1536,1]{1,2,0:T(1,128)S(1)} %bitcast.5), channel_id=1, replica_groups=mesh['gx'=32,'gy'=4] {'gx','gy'}, dimensions={0} | all-to-all | bytes 1572864 | tf_op jit(solution)/shard_map/all_to_all | solution.py:318
  29.6 0.0 copy-done
  29.6 0.0 copy-done.1
  29.6 4.8 %incident.1 = (f32[2,64,256]{2,1,0:T(8,128)S(1)}, f32[72,256]{1,0:T(8,128)S(1)}, f32[72,256]{1,0:T(8,128)S(1)}) custom-call(f32[1536,128]{1,0:T(8,128)S(1)} %bitcast.6, f32[2,64,256]{2,1,0:T(8,128)S(1)} %bitcast.11, f32[64,256]{1,0:T(8,128)S(1)} %bitcast.8), custom_call_target="tpu_custom_call" | custom-call | tf_op jit(solution)/shard_map/incident/pallas_call | solution.py:332
  34.5 0.6 %collective-permute-start = (f32[72,256]{1,0:T(8,128)S(1)}, f32[72,256]{1,0:T(8,128)S(1)}, u32[]{:S(2)}, u32[]{:S(2)}) collective-permute-start(f32[72,256]{1,0:T(8,128)S(1)} %get-tuple-element.13), channel_id=1, source_target_pairs={{0,4},{4,8},{8,12},{12,16},{16,20},{20,24},{24,28},{28,32},{32,36}... | collective-permute-start | bytes 221192 | tf_op jit(solution)/shard_map/ppermute | solution.py:345
  35.1 7.2 %collective-permute-start.1 = (f32[72,256]{1,0:T(8,128)S(1)}, f32[72,256]{1,0:T(8,128)S(1)}, u32[]{:S(2)}, u32[]{:S(2)}) collective-permute-start(f32[72,256]{1,0:T(8,128)S(1)} %get-tuple-element.14), channel_id=1, source_target_pairs={{4,0},{8,4},{12,8},{16,12},{20,16},{24,20},{28,24},{32,28},{36,32}... | collective-permute-start | bytes 221192 | tf_op jit(solution)/shard_map/ppermute | solution.py:346
  42.3 8.0 %coefficient.1 = (f32[4,64,256]{2,1,0:T(8,128)S(1)}, f32[32,256]{1,0:T(8,128)S(1)}, f32[32,256]{1,0:T(8,128)S(1)}) custom-call(f32[1536,128]{1,0:T(8,128)S(1)} %bitcast.7), custom_call_target="tpu_custom_call" | custom-call | flops 7516192768 | bytes 786432 | tf_op jit(solution)/shard_map/coefficient/pallas_call | solution.py:348
  50.3 0.0 collective-permute-done.above_ref
  50.3 0.0 collective-permute-done.1.below_ref
  50.4 0.2 strips.1
  50.6 0.1 collective-permute-start.4
  50.7 1.7 %collective-permute-start.5 = (f32[8,16,128]{2,1,0:T(8,128)S(1)}, f32[8,16,128]{2,1,0:T(8,128)S(1)}, u32[]{:S(2)}, u32[]{:S(2)}) collective-permute-start(f32[8,16,128]{2,1,0:T(8,128)S(1)} %get-tuple-element.19), channel_id=1, source_target_pairs={{1,0},{2,1},{3,2},{0,3},{5,4},{6,5},{7,6},{4,7},{9,8},{10,9},{11,1... | collective-permute-start | bytes 196616 | tf_op jit(solution)/shard_map/ppermute | solution.py:369
  52.4 0.0 collective-permute-start.2
  52.4 7.7 %collective-permute-start.3 = (f32[32,256]{1,0:T(8,128)S(1)}, f32[32,256]{1,0:T(8,128)S(1)}, u32[]{:S(2)}, u32[]{:S(2)}) collective-permute-start(f32[32,256]{1,0:T(8,128)S(1)} %get-tuple-element.17), channel_id=1, source_target_pairs={{4,0},{8,4},{12,8},{16,12},{20,16},{24,20},{28,24},{32,28},{36,32}... | collective-permute-start | bytes 98312 | tf_op jit(solution)/shard_map/ppermute | solution.py:359
  60.2 1.9 %collective-permute-done.2.above_ref = f32[32,256]{1,0:T(8,128)S(1)} collective-permute-done((f32[32,256]{1,0:T(8,128)S(1)}, f32[32,256]{1,0:T(8,128)S(1)}, u32[]{:S(2)}, u32[]{:S(2)}) %collective-permute-start.2) | collective-permute-done | bytes 32800 | tf_op jit(solution)/shard_map/ppermute | solution.py:358
  62.0 0.0 collective-permute-done.3.below_ref
  62.1 0.0 collective-permute-done.4.fleft_ref
  62.1 0.0 collective-permute-done.5.fright_ref
  62.1 1.8 %final.1 = (f32[2,8,8,256]{3,2,1,0:T(8,128)}, f32[2,8,8,256]{3,2,1,0:T(8,128)}) custom-call(f32[2,64,256]{2,1,0:T(8,128)S(1)} %get-tuple-element.11.r1_ref, f32[64,256]{1,0:T(8,128)S(1)} %bitcast.10, f32[4,64,256]{2,1,0:T(8,128)S(1)} %get-tuple-element.12.wn_ref, f32[3,2,64,128]{3,2,1,0:T(8,128)S(1)} %get-tuple-element.15.halo_ref, ...), custom_call_target="tpu_custom_call" | custom-call | tf_op jit(solution)/shard_map/final/pallas_call | solution.py:371
Async XLA Ops:
  2.3 27.3 %copy-start = (f32[8,8,256]{2,1,0:T(8,128)S(1)}, f32[8,8,256]{2,1,0:T(8,128)}, u32[]{:S(2)}) copy-start(f32[8,8,256]{2,1,0:T(8,128)} %param.9) | copy-start | bytes 196612
  2.4 27.3 %copy-start.1 = (f32[2,8,8,256]{3,2,1,0:T(8,128)S(1)}, f32[2,8,8,256]{3,2,1,0:T(8,128)}, u32[]{:S(2)}) copy-start(f32[2,8,8,256]{3,2,1,0:T(8,128)} %param.8) | copy-start | bytes 393220
  34.5 15.9 %collective-permute-start = (f32[72,256]{1,0:T(8,128)S(1)}, f32[72,256]{1,0:T(8,128)S(1)}, u32[]{:S(2)}, u32[]{:S(2)}) collective-permute-start(f32[72,256]{1,0:T(8,128)S(1)} %get-tuple-element.13), channel_id=1, source_target_pairs={{0,4},{4,8},{8,12},{12,16},{16,20},{20,24},{24,28},{28,32},{32,36}... | collective-permute-start | bytes 221192 | tf_op jit(solution)/shard_map/ppermute | solution.py:345
  35.1 15.2 %collective-permute-start.1 = (f32[72,256]{1,0:T(8,128)S(1)}, f32[72,256]{1,0:T(8,128)S(1)}, u32[]{:S(2)}, u32[]{:S(2)}) collective-permute-start(f32[72,256]{1,0:T(8,128)S(1)} %get-tuple-element.14), channel_id=1, source_target_pairs={{4,0},{8,4},{12,8},{16,12},{20,16},{24,20},{28,24},{32,28},{36,32}... | collective-permute-start | bytes 221192 | tf_op jit(solution)/shard_map/ppermute | solution.py:346
  50.6 11.5 %collective-permute-start.4 = (f32[8,16,128]{2,1,0:T(8,128)S(1)}, f32[8,16,128]{2,1,0:T(8,128)S(1)}, u32[]{:S(2)}, u32[]{:S(2)}) collective-permute-start(f32[8,16,128]{2,1,0:T(8,128)S(1)} %get-tuple-element.18), channel_id=1, source_target_pairs={{0,1},{1,2},{2,3},{3,0},{4,5},{5,6},{6,7},{7,4},{8,9},{9,10},{10,1... | collective-permute-start | bytes 196616 | tf_op jit(solution)/shard_map/ppermute | solution.py:368
  50.7 11.4 %collective-permute-start.5 = (f32[8,16,128]{2,1,0:T(8,128)S(1)}, f32[8,16,128]{2,1,0:T(8,128)S(1)}, u32[]{:S(2)}, u32[]{:S(2)}) collective-permute-start(f32[8,16,128]{2,1,0:T(8,128)S(1)} %get-tuple-element.19), channel_id=1, source_target_pairs={{1,0},{2,1},{3,2},{0,3},{5,4},{6,5},{7,6},{4,7},{9,8},{10,9},{11,1... | collective-permute-start | bytes 196616 | tf_op jit(solution)/shard_map/ppermute | solution.py:369
  52.4 9.6 %collective-permute-start.2 = (f32[32,256]{1,0:T(8,128)S(1)}, f32[32,256]{1,0:T(8,128)S(1)}, u32[]{:S(2)}, u32[]{:S(2)}) collective-permute-start(f32[32,256]{1,0:T(8,128)S(1)} %get-tuple-element.16), channel_id=1, source_target_pairs={{0,4},{4,8},{8,12},{12,16},{16,20},{20,24},{24,28},{28,32},{32,36}... | collective-permute-start | bytes 98312 | tf_op jit(solution)/shard_map/ppermute | solution.py:358
  52.4 9.6 %collective-permute-start.3 = (f32[32,256]{1,0:T(8,128)S(1)}, f32[32,256]{1,0:T(8,128)S(1)}, u32[]{:S(2)}, u32[]{:S(2)}) collective-permute-start(f32[32,256]{1,0:T(8,128)S(1)} %get-tuple-element.17), channel_id=1, source_target_pairs={{4,0},{8,4},{12,8},{16,12},{20,16},{24,20},{28,24},{32,28},{36,32}... | collective-permute-start | bytes 98312 | tf_op jit(solution)/shard_map/ppermute | solution.py:359
where the time goes:
time: 64 us; the launch traced here: 63.9 us
  blocking collectives  27.2 us (42%)
  starting transfers between devices  17.4 us (27%)
  Pallas kernels  16.6 us (26%)
  waiting for transfers between devices  1.9 us (3%)
  between operations  0.71 us (1%)
    all_to_all x1, blocking collectives, per_device(): lax.all_to_all(send.reshape(-1), ('gx', 'gy'), split_axis=0, concat_axis=...  27.2 us
    pallas_call x1, Pallas kernels, per_device(): pl.pallas_call(coefficient_kernel, out_shape=(shape(4, cells, cols), shap...  8.05 us
    ppermute x1, starting transfers between devices, per_device(): below_wn = lax.ppermute(up, 'gx', before_x)  7.75 us
    ppermute x1, starting transfers between devices, per_device(): below = lax.ppermute(up, 'gx', before_x)  7.17 us
    pallas_call x1, Pallas kernels, per_device(): pl.pallas_call(incident_kernel, out_shape=(shape(2, cells, cols), shape(9...  4.83 us
    ppermute x1, waiting for transfers between devices, per_device(): above_wn = lax.ppermute(down, 'gx', after_x)  1.89 us
    pallas_call x1, Pallas kernels, per_device(): pl.pallas_call(final_kernel, out_shape=(field, field), in_specs=in_vmem(8...  1.81 us
    ppermute x1, starting transfers between devices, per_device(): from_right = lax.ppermute(to_left, 'gy', before_y)  1.73 us
  transfers between devices with their start and end apart: 6, of which 1 were waited for; matrix products, arithmetic and copies ran while one was open for 0% of the time, Pallas kernels for 13%

commit v1 on v0

v1 whole, which is shorter than its diff:
```python
import functools

import jax
import jax.numpy as jnp
from jax import lax
from jax.experimental import pallas as pl
from jax.experimental.pallas import tpu as pltpu
from jax.sharding import PartitionSpec as P

CAP = 2
K_SQUARED = 0.25
BETA = 0.5
OMEGA = 0.8
TAU = 1.0

CHANNELS = 6
GROUP = 128

f32 = jnp.float32
bf16 = jnp.bfloat16


def pack_kernel(
    owner_hbm, dist_hbm, normal_hbm, inc_hbm, cell_hbm, mask_hbm, out_ref,
    owner_ref, base_ref, count_ref, dist_ref, coef_ref, cell_ref, mask_ref, sems,
):
    blocks = dist_ref.shape[0]
    devices = count_ref.shape[0]
    copies = [
        pltpu.make_async_copy(owner_hbm, owner_ref, sems.at[0]),
        pltpu.make_async_copy(dist_hbm, dist_ref, sems.at[1]),
        pltpu.make_async_copy(normal_hbm, coef_ref.at[pl.ds(0, 3)], sems.at[2]),
        pltpu.make_async_copy(inc_hbm, coef_ref.at[pl.ds(3, 2)], sems.at[3]),
        pltpu.make_async_copy(cell_hbm, cell_ref, sems.at[4]),
        pltpu.make_async_copy(mask_hbm, mask_ref, sems.at[5]),
    ]
    for copy in copies:
        copy.start()
    out_ref[...] = jnp.full(out_ref.shape, -1.0, f32)

    def clear(i, carry):
        count_ref[i] = 0
        return carry

    lax.fori_loop(0, devices, clear, 0, unroll=8)
    copies[0].wait()

    def rank(b, carry):
        owner = owner_ref[b]
        seen = count_ref[owner]
        count_ref[owner] = seen + 1
        base_ref[b] = (owner * CAP + seen) * CHANNELS
        return carry

    lax.fori_loop(0, blocks, rank, 0, unroll=8)
    for copy in copies[1:]:
        copy.wait()
    half = 0.5 * TAU * dist_ref[...]
    for k in range(3):
        coef_ref[k] = half * coef_ref[k]
    for k in range(3, 5):
        coef_ref[k] = TAU * coef_ref[k]
    coef_ref[5] = jnp.where(mask_ref[...] > 0, cell_ref[...], 1 << 14).astype(f32)

    def place(b, carry):
        base = base_ref[b]
        for c in range(CHANNELS):
            out_ref[pl.ds(base + c, 1), :] = coef_ref[c, pl.ds(b, 1), :]
        return carry

    lax.fori_loop(0, blocks, place, 0, unroll=8)


def scatter_slots(recv_ref, hi_ref, lo_ref, acc_ref, groups):
    slots = hi_ref.shape[0]
    lo_n = acc_ref.shape[1]
    per_step = min(GROUP, slots)
    chunk = min(64, slots)
    for i in range(0, slots, chunk):
        cell = recv_ref[pl.ds(i * CHANNELS + CHANNELS - 1, chunk, stride=CHANNELS), :].astype(jnp.int32)
        hi_ref[i : i + chunk] = (cell >> 8).astype(f32)
        lo_ref[i : i + chunk] = (cell & 255).astype(f32)
    acc_ref[...] = jnp.zeros(acc_ref.shape, f32)
    one = jnp.ones((), bf16)
    zero = jnp.zeros((), bf16)
    targets = []
    for rows, _, _ in groups:
        place = lax.broadcasted_iota(jnp.int32, (8 * len(rows), 128), 0)
        item = place >> 3
        row = jnp.zeros_like(place)
        for k, r in enumerate(rows):
            row = jnp.where(item == k, r, row)
        targets.append(((place & 7) * 8 + row).astype(f32).astype(bf16))
    lo_iota = lax.broadcasted_iota(jnp.int32, (lo_n, 128), 0).astype(f32).astype(bf16)

    def load(ref, index):
        return jnp.broadcast_to(ref[pl.ds(index, 1), :], (16, 128))

    def tall(tile, n):
        return jnp.concatenate([tile] * (n // 16), axis=0)

    def step(g, carry):
        left, right = [], []
        for j in range(per_step):
            slot = g * per_step + j
            hi = load(hi_ref, slot).astype(bf16)
            pieces = []
            for target, (rows, channels, count) in zip(targets, groups):
                n = 8 * len(rows)
                hot = target == tall(hi, n)
                for c in channels:
                    value = load(recv_ref, slot * CHANNELS + c)
                    lead = value.astype(bf16)
                    rest = (value - lead.astype(f32)).astype(bf16)
                    pieces.append(jnp.where(hot, tall(lead, n), zero))
                    pieces.append(jnp.where(hot, tall(rest, n), zero))
                if count:
                    pieces.append(jnp.where(hot, one, zero))
            left.append(jnp.concatenate(pieces, axis=0))
            right.append(jnp.where(lo_iota == tall(load(lo_ref, slot).astype(bf16), lo_n), one, zero))
        acc_ref[...] += lax.dot_general(
            jnp.concatenate(left, axis=1),
            jnp.concatenate(right, axis=1),
            (((1,), (1,)), ((), ())),
            preferred_element_type=f32,
        )
        return carry

    lax.fori_loop(0, slots // per_step, step, 0)
    sums, start = [], 0
    for rows, channels, count in groups:
        n = 8 * len(rows)
        found = []
        for _ in channels:
            found.append(acc_ref[start : start + n, :] + acc_ref[start + n : start + 2 * n, :])
            start += 2 * n
        if count:
            found.append(acc_ref[start : start + n, :])
            start += n
        sums.append(found)
    return sums


def keep_tiles(ref, k, value):
    for t in range(ref.shape[1]):
        ref[k, t] = value[:, t * 128 : (t + 1) * 128]


def load_rows(ref, k, t, row):
    return ref[k, t, pl.ds(row, ref.shape[2] // 8, stride=8), :]


def store_rows(ref, k, row, value):
    for t in range(ref.shape[1]):
        ref[k, t, pl.ds(row, ref.shape[2] // 8, stride=8), :] = value[:, t * 128 : (t + 1) * 128]


ALL = tuple(range(8))
EDGES = (0, 7)
INNER = (1, 2, 3, 4, 5, 6)
FIELDS = ((0, 1, 2), True)


def first_kernel(
    recv_ref, rhs_ref, perm_ref, r1_ref, edge_ref, pair_ref, other_ref, hi_ref, lo_ref, acc_ref, tile_ref
):
    incident, fields = scatter_slots(recv_ref, hi_ref, lo_ref, acc_ref, ((ALL, (3, 4), False), (EDGES,) + FIELDS))
    planes = perm_ref.shape[0] // 8
    for k in range(2):
        for r in range(8):
            store_rows(tile_ref, k, r, incident[k][r * planes : (r + 1) * planes])
    for k in range(2):
        inc = jnp.concatenate([tile_ref[k, t] for t in range(tile_ref.shape[1])], axis=1)
        value = rhs_ref[k] - inc
        r1_ref[k] = value
        keep_tiles(tile_ref, k, value)
    keep_tiles(tile_ref, 2, perm_ref[...])
    fields = [TAU * fields[3]] + fields[:3]
    for k in range(4):
        edge_ref[k] = fields[k]
    place = lax.axis_index("gx")
    even = lax.rem(place, 2) == 0
    top, bottom = place == 0, place == lax.axis_size("gx") - 1
    for t in range(tile_ref.shape[1]):
        lanes = slice(t * 128, (t + 1) * 128)
        for c in range(7):
            for k in range(3 if c < 3 else 1):
                if c < 3:
                    item = 3 * c + k
                    first, last = load_rows(tile_ref, c, t, k), load_rows(tile_ref, c, t, 5 + k)
                else:
                    item = 6 + c
                    first, last = fields[c - 3][0:planes, lanes], fields[c - 3][planes : 2 * planes, lanes]
                if c == 2:
                    first, last = jnp.where(top, 0.0, first), jnp.where(bottom, 0.0, last)
                rows = slice(item * planes, (item + 1) * planes)
                pair_ref[rows, lanes] = jnp.where(even, last, first)
                other_ref[rows, lanes] = jnp.where(even, first, last)


def second_kernel(recv_ref, edge_ref, wn_ref, hi_ref, lo_ref, acc_ref):
    (fields,) = scatter_slots(recv_ref, hi_ref, lo_ref, acc_ref, ((INNER,) + FIELDS,))
    planes = edge_ref.shape[1] // 2
    for k, value in enumerate([TAU * fields[3]] + fields[:3]):
        for j, r in enumerate(EDGES):
            store_rows(wn_ref, k, r, edge_ref[k, j * planes : (j + 1) * planes])
        for j, r in enumerate(INNER):
            store_rows(wn_ref, k, r, value[j * planes : (j + 1) * planes])


COL_PLACE = ((0, 3), (3, 3), (6, 3), (9, 1), (10, 1), (11, 1), (12, 1))


def strip_kernel(r1_ref, perm_ref, wn_ref, pair_ref, other_ref, out_pair_ref, out_other_ref, halo_ref):
    planes = perm_ref.shape[0] // 8
    lo_n = perm_ref.shape[1]
    even = lax.rem(lax.axis_index("gx"), 2) == 0
    halo_ref[...] = jnp.zeros(halo_ref.shape, f32)
    for c in range(7):
        width = 3 if c < 3 else 1
        for k in range(width):
            item = 3 * c + k if c < 3 else 6 + c
            rows = slice(item * planes, (item + 1) * planes)
            pair, other = pair_ref[rows, :], other_ref[rows, :]
            store_rows(halo_ref, c, k, jnp.where(even, pair, other))
            store_rows(halo_ref, c, 8 - width + k, jnp.where(even, other, pair))
    lane = lax.broadcasted_iota(jnp.int32, (planes, 16, 128), 2)
    position = lax.axis_index("gy")
    even = lax.rem(position, 2) == 0
    last = lax.axis_size("gy") - 1
    nothing = jnp.zeros((planes, 8, 128), f32)
    strips = []
    for start, sign, edge in ((0, 1, 0), (lo_n - 128, -1, last)):
        place = lane if sign > 0 else 127 - lane
        strip = jnp.zeros((planes, 16, 128), f32)
        for c in range(7):
            if c < 3:
                own = perm_ref[:, pl.ds(start, 128)] if c == 2 else r1_ref[c, :, pl.ds(start, 128)]
                other = halo_ref[c, start // 128].reshape(planes, 8, 128)
            else:
                own, other = wn_ref[c - 3, start // 128], nothing
            full = jnp.concatenate([own.reshape(planes, 8, 128), other], axis=1)
            offset, width = COL_PLACE[c]
            moved = pltpu.roll(full, (sign * offset) % 128, axis=2)
            strip = jnp.where((place >= offset) & (place < offset + width), moved, strip)
        strips.append(jnp.where(position == edge, 0.0, strip))
    out_pair_ref[...] = jnp.where(even, strips[1], strips[0])
    out_other_ref[...] = jnp.where(even, strips[0], strips[1])


def final_kernel(r1_ref, perm_ref, wn_ref, halo_ref, pair_ref, other_ref, sol_ref, res_ref):
    planes = perm_ref.shape[0] // 8
    lo_n = perm_ref.shape[1]
    wide = lo_n + 128
    lane = lax.broadcasted_iota(jnp.int32, (planes, 16, 128), 2)
    even = lax.rem(lax.axis_index("gy"), 2) == 0
    pair, other_pair = pair_ref[...], other_ref[...]
    from_right = jnp.where(even, pair, other_pair)
    from_left = jnp.where(even, other_pair, pair)

    def joined(ref, k):
        tiles = [ref[k, t].reshape(planes, 8, 128) for t in range(lo_n // 128)]
        return jnp.concatenate(tiles, axis=2)

    def extended(c):
        if c < 3:
            own = (perm_ref[...] if c == 2 else r1_ref[c]).reshape(planes, 8, lo_n)
        else:
            own = joined(wn_ref, c - 3)
        body = jnp.concatenate([own, joined(halo_ref, c)], axis=1)
        offset, width = COL_PLACE[c]
        right = pltpu.roll(from_right, (-offset) % 128, axis=2)
        left = pltpu.roll(from_left, offset, axis=2)
        side = jnp.where(lane < width, right, jnp.where(lane >= 128 - width, left, 0.0))
        return jnp.concatenate([body, side], axis=2)

    re, im, perm, w, nz, nx, ny = [extended(c) for c in range(7)]
    diag = 6.0 - K_SQUARED * perm
    shift = BETA * K_SQUARED * perm
    denom = diag * diag + shift * shift
    inside = perm > 0.5
    inv_re = jnp.where(inside, OMEGA * diag / denom, 0.0)
    inv_im = jnp.where(inside, -OMEGA * shift / denom, 0.0)

    def damp(a, b):
        return a * inv_re - b * inv_im, a * inv_im + b * inv_re

    def sides(v):
        nothing = jnp.zeros((1,) + v.shape[1:], f32)
        after = jnp.concatenate([v[1:], nothing], axis=0)
        before = jnp.concatenate([nothing, v[:-1]], axis=0)
        return (
            (after, before),
            (pltpu.roll(v, 15, axis=1), pltpu.roll(v, 1, axis=1)),
            (pltpu.roll(v, wide - 1, axis=2), pltpu.roll(v, 1, axis=2)),
        )

    def helm(v, pairs):
        total = pairs[0][0] + pairs[0][1]
        for a, b in pairs[1:]:
            total = total + a + b
        return diag * v - total

    def swept(a, b):
        za, zb = damp(a, b)
        ma = helm(za, sides(za)) - shift * zb
        mb = helm(zb, sides(zb)) + shift * za
        da, db = damp(a - ma, b - mb)
        return za + da, zb + db

    def surface(v, pairs):
        (a, b), (c, d), (e, f) = pairs
        return w * v + nz * (a - b) + nx * (c - d) + ny * (e - f)

    def remaining(r, v):
        pairs = sides(v)
        return r - helm(v, pairs) - surface(v, pairs)

    sa, sb = swept(re, im)
    ra, rb = remaining(re, sa), remaining(im, sb)
    ua, ub = swept(ra, rb)
    res_ref[0] = ra[:, 0:8, 0:lo_n]
    res_ref[1] = rb[:, 0:8, 0:lo_n]
    sol_ref[0] = (sa + ua)[:, 0:8, 0:lo_n]
    sol_ref[1] = (sb + ub)[:, 0:8, 0:lo_n]


def in_vmem(n):
    return [pl.BlockSpec(memory_space=pltpu.VMEM)] * n


def shape(*dims):
    return jax.ShapeDtypeStruct(dims, f32)


def per_device(rhs_field, permittivity, surf_dist, surf_normal, surf_inc, surf_cell, surf_mask, surf_owner):
    planes, rows, cols = permittivity.shape
    blocks, points = surf_cell.shape
    gx, gy = lax.axis_size("gx"), lax.axis_size("gy")
    devices = gx * gy
    slots = devices * CAP
    params = pltpu.CompilerParams(vmem_limit_bytes=48 << 20)
    send = pl.pallas_call(
        pack_kernel,
        out_shape=shape(slots * CHANNELS, points),
        in_specs=[pl.BlockSpec(memory_space=pltpu.HBM)] * 6,
        out_specs=pl.BlockSpec(memory_space=pltpu.VMEM),
        scratch_shapes=[
            pltpu.SMEM((blocks,), jnp.int32),
            pltpu.SMEM((blocks,), jnp.int32),
            pltpu.SMEM((devices,), jnp.int32),
            pltpu.VMEM((blocks, points), f32),
            pltpu.VMEM((CHANNELS, blocks, points), f32),
            pltpu.VMEM((blocks, points), jnp.int32),
            pltpu.VMEM((blocks, points), jnp.int32),
            pltpu.SemaphoreType.DMA((6,)),
        ],
        compiler_params=params,
        name="pack",
    )(*[
        pltpu.with_memory_space_constraint(x, pltpu.HBM)
        for x in (surf_owner[:, 0], surf_dist, surf_normal, surf_inc, surf_cell, surf_mask)
    ])
    recv = lax.all_to_all(send.reshape(-1), ("gx", "gy"), split_axis=0, concat_axis=0, tiled=True)
    recv = recv.reshape(slots * CHANNELS, points)
    cells = planes * rows
    rhs_field = rhs_field.reshape(2, cells, cols)
    permittivity = permittivity.reshape(cells, cols)

    tiles = cols // 128

    def scatter_scratch(parts):
        return [
            pltpu.VMEM((slots, points), f32),
            pltpu.VMEM((slots, points), f32),
            pltpu.VMEM((parts, cols), f32),
        ]

    def cost(parts):
        flops = 2 * parts * cols * slots * points
        return pl.CostEstimate(flops=flops, transcendentals=0, bytes_accessed=slots * CHANNELS * points * 4)

    strip = shape(13 * planes, cols)
    parts = 4 * cells + 14 * planes
    r1, edges, pair, other = pl.pallas_call(
        first_kernel,
        out_shape=(shape(2, cells, cols), shape(4, 2 * planes, cols), strip, strip),
        in_specs=in_vmem(3),
        out_specs=tuple(in_vmem(4)),
        scratch_shapes=scatter_scratch(parts) + [pltpu.VMEM((3, tiles, cells, 128), f32)],
        compiler_params=params,
        cost_estimate=cost(parts),
        name="first",
    )(recv, rhs_field, permittivity)
    from_pair = lax.ppermute(pair, "gx", [(i, i ^ 1) for i in range(gx)])
    from_other = lax.ppermute(other, "gx", [(i, (((i + 1) ^ 1) - 1) % gx) for i in range(gx)])
    parts = 7 * 6 * planes
    wn = pl.pallas_call(
        second_kernel,
        out_shape=shape(4, tiles, cells, 128),
        in_specs=in_vmem(2),
        out_specs=in_vmem(1)[0],
        scratch_shapes=scatter_scratch(parts),
        compiler_params=params,
        cost_estimate=cost(parts),
        name="second",
    )(recv, edges)
    pair, other, halo = pl.pallas_call(
        strip_kernel,
        out_shape=(shape(planes, 16, 128), shape(planes, 16, 128), shape(7, tiles, cells, 128)),
        in_specs=in_vmem(5),
        out_specs=tuple(in_vmem(3)),
        compiler_params=params,
        name="strips",
    )(r1, permittivity, wn, from_pair, from_other)
    from_pair = lax.ppermute(pair, "gy", [(i, i ^ 1) for i in range(gy)])
    from_other = lax.ppermute(other, "gy", [(i, (((i + 1) ^ 1) - 1) % gy) for i in range(gy)])
    field = shape(2, planes, rows, cols)
    return pl.pallas_call(
        final_kernel,
        out_shape=(field, field),
        in_specs=in_vmem(6),
        out_specs=tuple(in_vmem(2)),
        compiler_params=params,
        name="final",
    )(r1, permittivity, wn, halo, from_pair, from_other)


def solution(mesh):
    split = ("gx", "gy")
    placed = (
        P(None, None, "gx", "gy"),
        P(None, "gx", "gy"),
        P(split, None),
        P(None, split, None),
        P(None, split, None),
        P(split, None),
        P(split, None),
        P(split, None),
    )
    return jax.shard_map(
        per_device,
        mesh=mesh,
        in_specs=placed,
        out_specs=(P(None, None, "gx", "gy"), P(None, None, "gx", "gy")),
        check_vma=False,
    )
```

time: 64 us -> 55 us (0.86)
  the two profiles are of different devices: /device:TPU:0 before, /device:TPU:1 now
where the time goes in v1:
time: 55 us; the launch traced here: 54.8 us
  blocking collectives  27.4 us (50%)
  Pallas kernels  16.7 us (30%)
  starting transfers between devices  6.56 us (12%)
  waiting for transfers between devices  3.44 us (6%)
  between operations  0.69 us (1%)
    all_to_all x1, blocking collectives, per_device(): lax.all_to_all(send.reshape(-1), ('gx', 'gy'), split_axis=0, concat_axis=...  27.4 us
    pallas_call x1, Pallas kernels, per_device(): pl.pallas_call(first_kernel, out_shape=(shape(2, cells, cols), shape(4, 2...  6.76 us
    pallas_call x1, Pallas kernels, per_device(): pl.pallas_call(second_kernel, out_shape=shape(4, tiles, cells, 128), in_s...  6.16 us
    ppermute x1, starting transfers between devices, per_device(): lax.ppermute(other, 'gx', [(i, ((i + 1 ^ 1) - 1) % gx) for i in range(gx)])  3.08 us
    ppermute x1, waiting for transfers between devices, per_device(): lax.ppermute(other, 'gy', [(i, ((i + 1 ^ 1) - 1) % gy) for i in range(gy)])  2.89 us
    ppermute x1, starting transfers between devices, per_device(): from_pair = lax.ppermute(pair, 'gy', [(i, i ^ 1) for i in range(gy)])  2.24 us
    pallas_call x1, Pallas kernels, per_device(): pl.pallas_call(final_kernel, out_shape=(field, field), in_specs=in_vmem(6...  1.79 us
    pallas_call x1, Pallas kernels, per_device(): pl.pallas_call(pack_kernel, out_shape=shape(slots * CHANNELS, points), in...  1.71 us
  transfers between devices with their start and end apart: 4, of which 2 were waited for; matrix products, arithmetic and copies ran while one was open for 0% of the time, Pallas kernels for 11%

profile of v1, /device:TPU:1, one launch (start us, length us, event | category | flops | bytes accessed | tf_op | source)
XLA Modules:
  0.0 54.8 jit_solution(5858070288173196046)
XLA Ops:
  0.6 1.7 %pack.1 = f32[1536,128]{1,0:T(8,128)S(1)} custom-call(s32[128]{0:T(128)} %bitcast.12, f32[128,128]{1,0:T(8,128)} %dist_hbm.1, f32[3,128,128]{2,1,0:T(8,128)} %normal_hbm.1, f32[2,128,128]{2,1,0:T(8,128)} %inc_hbm.1, s32[128,128]{1,0:T(8,128)} %cell_hbm.1, s32[128,128]{1,0:T(8,128)} %mask_hbm.1), custom_call_target="tpu_custom_call" | custom-call | tf_op jit(solution)/shard_map/pack/pallas_call | solution.py:343
  2.3 0.0 copy-start
  2.4 0.0 copy-start.1
  2.4 27.4 %all_to_all.9 = f32[128,1536,1]{1,2,0:T(1,128)S(1)} all-to-all(f32[128,1536,1]{1,2,0:T(1,128)S(1)} %bitcast.5), channel_id=1, replica_groups=mesh['gx'=32,'gy'=4] {'gx','gy'}, dimensions={0} | all-to-all | bytes 1572864 | tf_op jit(solution)/shard_map/all_to_all | solution.py:364
  29.8 0.0 copy-done
  29.8 0.0 copy-done.1
  29.8 6.8 %first.1 = (f32[2,64,256]{2,1,0:T(8,128)S(1)}, f32[4,16,256]{2,1,0:T(8,128)S(1)}, f32[104,256]{1,0:T(8,128)S(1)}, f32[104,256]{1,0:T(8,128)S(1)}) custom-call(f32[1536,128]{1,0:T(8,128)S(1)} %bitcast.6, f32[2,64,256]{2,1,0:T(8,128)S(1)} %bitcast.11, f32[64,256]{1,0:T(8,128)S(1)} %bitcast.8), custom_call_target="tpu_custom_call" | custom-call | flops 6174015488 | bytes 786432 | tf_op jit(solution)/shard_map/first/pallas_call | solution.py:385
  36.6 0.9 %collective-permute-start = (f32[104,256]{1,0:T(8,128)S(1)}, f32[104,256]{1,0:T(8,128)S(1)}, u32[]{:S(2)}, u32[]{:S(2)}) collective-permute-start(f32[104,256]{1,0:T(8,128)S(1)} %get-tuple-element.11), channel_id=1, source_target_pairs={{0,4},{4,0},{8,12},{12,8},{16,20},{20,16},{24,28},{28,24},{32,36},... | collective-permute-start | bytes 319496 | tf_op jit(solution)/shard_map/ppermute | solution.py:395
  37.5 3.1 %collective-permute-start.1 = (f32[104,256]{1,0:T(8,128)S(1)}, f32[104,256]{1,0:T(8,128)S(1)}, u32[]{:S(2)}, u32[]{:S(2)}) collective-permute-start(f32[104,256]{1,0:T(8,128)S(1)} %get-tuple-element.12), channel_id=1, source_target_pairs={{0,124},{4,8},{8,4},{12,16},{16,12},{20,24},{24,20},{28,32},{32,28... | collective-permute-start | bytes 319496 | tf_op jit(solution)/shard_map/ppermute | solution.py:396
  40.6 6.2 %second.1.wn_ref = f32[4,2,64,128]{3,2,1,0:T(8,128)S(1)} custom-call(f32[1536,128]{1,0:T(8,128)S(1)} %bitcast.7, f32[4,16,256]{2,1,0:T(8,128)S(1)} %get-tuple-element.10.edge_ref), custom_call_target="tpu_custom_call" | custom-call | flops 5637144576 | bytes 786432 | tf_op jit(solution)/shard_map/second/pallas_call | solution.py:398
  46.7 0.0 collective-permute-done.pair_ref
  46.7 0.0 collective-permute-done.1.other_ref
  46.7 0.3 strips.1
  47.0 2.2 %collective-permute-start.2 = (f32[8,16,128]{2,1,0:T(8,128)S(1)}, f32[8,16,128]{2,1,0:T(8,128)S(1)}, u32[]{:S(2)}, u32[]{:S(2)}) collective-permute-start(f32[8,16,128]{2,1,0:T(8,128)S(1)} %get-tuple-element.14), channel_id=1, source_target_pairs={{0,1},{1,0},{2,3},{3,2},{4,5},{5,4},{6,7},{7,6},{8,9},{9,8},{10,11... | collective-permute-start | bytes 196616 | tf_op jit(solution)/shard_map/ppermute | solution.py:416
  49.2 0.4 collective-permute-start.3
  49.6 0.5 collective-permute-done.2.pair_ref
  50.1 2.9 %collective-permute-done.3.other_ref = f32[8,16,128]{2,1,0:T(8,128)S(1)} collective-permute-done((f32[8,16,128]{2,1,0:T(8,128)S(1)}, f32[8,16,128]{2,1,0:T(8,128)S(1)}, u32[]{:S(2)}, u32[]{:S(2)}) %collective-permute-start.3) | collective-permute-done | bytes 65568 | tf_op jit(solution)/shard_map/ppermute | solution.py:417
  53.0 1.8 %final.1 = (f32[2,8,8,256]{3,2,1,0:T(8,128)}, f32[2,8,8,256]{3,2,1,0:T(8,128)}) custom-call(f32[2,64,256]{2,1,0:T(8,128)S(1)} %get-tuple-element.9.r1_ref, f32[64,256]{1,0:T(8,128)S(1)} %bitcast.10, f32[4,2,64,128]{3,2,1,0:T(8,128)S(1)} %second.1.wn_ref, f32[7,2,64,128]{3,2,1,0:T(8,128)S(1)} %get-tuple-element.13.halo_ref, ...), custom_call_target="tpu_custom_call" | custom-call | tf_op jit(solution)/shard_map/final/pallas_call | solution.py:419
Async XLA Ops:
  2.3 27.5 %copy-start = (f32[8,8,256]{2,1,0:T(8,128)S(1)}, f32[8,8,256]{2,1,0:T(8,128)}, u32[]{:S(2)}) copy-start(f32[8,8,256]{2,1,0:T(8,128)} %param.9) | copy-start | bytes 196612
  2.4 27.5 %copy-start.1 = (f32[2,8,8,256]{3,2,1,0:T(8,128)S(1)}, f32[2,8,8,256]{3,2,1,0:T(8,128)}, u32[]{:S(2)}) copy-start(f32[2,8,8,256]{3,2,1,0:T(8,128)} %param.8) | copy-start | bytes 393220
  36.6 10.1 %collective-permute-start = (f32[104,256]{1,0:T(8,128)S(1)}, f32[104,256]{1,0:T(8,128)S(1)}, u32[]{:S(2)}, u32[]{:S(2)}) collective-permute-start(f32[104,256]{1,0:T(8,128)S(1)} %get-tuple-element.11), channel_id=1, source_target_pairs={{0,4},{4,0},{8,12},{12,8},{16,20},{20,16},{24,28},{28,24},{32,36},... | collective-permute-start | bytes 319496 | tf_op jit(solution)/shard_map/ppermute | solution.py:395
  37.5 9.3 %collective-permute-start.1 = (f32[104,256]{1,0:T(8,128)S(1)}, f32[104,256]{1,0:T(8,128)S(1)}, u32[]{:S(2)}, u32[]{:S(2)}) collective-permute-start(f32[104,256]{1,0:T(8,128)S(1)} %get-tuple-element.12), channel_id=1, source_target_pairs={{0,124},{4,8},{8,4},{12,16},{16,12},{20,24},{24,20},{28,32},{32,28... | collective-permute-start | bytes 319496 | tf_op jit(solution)/shard_map/ppermute | solution.py:396
  47.0 3.1 %collective-permute-start.2 = (f32[8,16,128]{2,1,0:T(8,128)S(1)}, f32[8,16,128]{2,1,0:T(8,128)S(1)}, u32[]{:S(2)}, u32[]{:S(2)}) collective-permute-start(f32[8,16,128]{2,1,0:T(8,128)S(1)} %get-tuple-element.14), channel_id=1, source_target_pairs={{0,1},{1,0},{2,3},{3,2},{4,5},{5,4},{6,7},{7,6},{8,9},{9,8},{10,11... | collective-permute-start | bytes 196616 | tf_op jit(solution)/shard_map/ppermute | solution.py:416
  49.2 3.8 %collective-permute-start.3 = (f32[8,16,128]{2,1,0:T(8,128)S(1)}, f32[8,16,128]{2,1,0:T(8,128)S(1)}, u32[]{:S(2)}, u32[]{:S(2)}) collective-permute-start(f32[8,16,128]{2,1,0:T(8,128)S(1)} %get-tuple-element.15), channel_id=1, source_target_pairs={{0,3},{1,2},{2,1},{3,0},{4,7},{5,6},{6,5},{7,4},{8,11},{9,10},{10,... | collective-permute-start | bytes 196616 | tf_op jit(solution)/shard_map/ppermute | solution.py:417

commit v2 on v1

--- a/solution.py
+++ b/solution.py
@@ -71,16 +71,19 @@
     lax.fori_loop(0, blocks, place, 0, unroll=8)
 
 
-def scatter_slots(recv_ref, hi_ref, lo_ref, acc_ref, groups):
+def split_cells(recv_ref, hi_ref, lo_ref):
     slots = hi_ref.shape[0]
-    lo_n = acc_ref.shape[1]
-    per_step = min(GROUP, slots)
     chunk = min(64, slots)
     for i in range(0, slots, chunk):
         cell = recv_ref[pl.ds(i * CHANNELS + CHANNELS - 1, chunk, stride=CHANNELS), :].astype(jnp.int32)
         hi_ref[i : i + chunk] = (cell >> 8).astype(f32)
         lo_ref[i : i + chunk] = (cell & 255).astype(f32)
-    acc_ref[...] = jnp.zeros(acc_ref.shape, f32)
+
+
+def scatter_slots(recv_ref, hi_ref, lo_ref, acc_ref, groups):
+    slots = hi_ref.shape[0]
+    lo_n = acc_ref.shape[1]
+    per_step = min(GROUP, slots)
     one = jnp.ones((), bf16)
     zero = jnp.zeros((), bf16)
     targets = []
@@ -99,7 +102,7 @@
     def tall(tile, n):
         return jnp.concatenate([tile] * (n // 16), axis=0)
 
-    def step(g, carry):
+    def step(g):
         left, right = [], []
         for j in range(per_step):
             slot = g * per_step + j
@@ -118,15 +121,16 @@
                     pieces.append(jnp.where(hot, one, zero))
             left.append(jnp.concatenate(pieces, axis=0))
             right.append(jnp.where(lo_iota == tall(load(lo_ref, slot).astype(bf16), lo_n), one, zero))
-        acc_ref[...] += lax.dot_general(
+        total = lax.dot_general(
             jnp.concatenate(left, axis=1),
             jnp.concatenate(right, axis=1),
             (((1,), (1,)), ((), ())),
             preferred_element_type=f32,
         )
-        return carry
-
-    lax.fori_loop(0, slots // per_step, step, 0)
+        acc_ref[...] = total if g == 0 else acc_ref[...] + total
+
+    for g in range(slots // per_step):
+        step(g)
     sums, start = [], 0
     for rows, channels, count in groups:
         n = 8 * len(rows)
@@ -164,6 +168,7 @@
 def first_kernel(
     recv_ref, rhs_ref, perm_ref, r1_ref, edge_ref, pair_ref, other_ref, hi_ref, lo_ref, acc_ref, tile_ref
 ):
+    split_cells(recv_ref, hi_ref, lo_ref)
     incident, fields = scatter_slots(recv_ref, hi_ref, lo_ref, acc_ref, ((ALL, (3, 4), False), (EDGES,) + FIELDS))
     planes = perm_ref.shape[0] // 8
     for k in range(2):
@@ -198,7 +203,7 @@
                 other_ref[rows, lanes] = jnp.where(even, first, last)
 
 
-def second_kernel(recv_ref, edge_ref, wn_ref, hi_ref, lo_ref, acc_ref):
+def second_kernel(recv_ref, hi_ref, lo_ref, edge_ref, wn_ref, acc_ref):
     (fields,) = scatter_slots(recv_ref, hi_ref, lo_ref, acc_ref, ((INNER,) + FIELDS,))
     planes = edge_ref.shape[1] // 2
     for k, value in enumerate([TAU * fields[3]] + fields[:3]):
@@ -248,39 +253,14 @@
     out_other_ref[...] = jnp.where(even, strips[0], strips[1])
 
 
-def final_kernel(r1_ref, perm_ref, wn_ref, halo_ref, pair_ref, other_ref, sol_ref, res_ref):
-    planes = perm_ref.shape[0] // 8
-    lo_n = perm_ref.shape[1]
-    wide = lo_n + 128
-    lane = lax.broadcasted_iota(jnp.int32, (planes, 16, 128), 2)
-    even = lax.rem(lax.axis_index("gy"), 2) == 0
-    pair, other_pair = pair_ref[...], other_ref[...]
-    from_right = jnp.where(even, pair, other_pair)
-    from_left = jnp.where(even, other_pair, pair)
-
-    def joined(ref, k):
-        tiles = [ref[k, t].reshape(planes, 8, 128) for t in range(lo_n // 128)]
-        return jnp.concatenate(tiles, axis=2)
-
-    def extended(c):
-        if c < 3:
-            own = (perm_ref[...] if c == 2 else r1_ref[c]).reshape(planes, 8, lo_n)
-        else:
-            own = joined(wn_ref, c - 3)
-        body = jnp.concatenate([own, joined(halo_ref, c)], axis=1)
-        offset, width = COL_PLACE[c]
-        right = pltpu.roll(from_right, (-offset) % 128, axis=2)
-        left = pltpu.roll(from_left, offset, axis=2)
-        side = jnp.where(lane < width, right, jnp.where(lane >= 128 - width, left, 0.0))
-        return jnp.concatenate([body, side], axis=2)
-
-    re, im, perm, w, nz, nx, ny = [extended(c) for c in range(7)]
+def iterate(re, im, perm, w, nz, nx, ny):
+    rows, cols = perm.shape[1:]
     diag = 6.0 - K_SQUARED * perm
     shift = BETA * K_SQUARED * perm
-    denom = diag * diag + shift * shift
     inside = perm > 0.5
-    inv_re = jnp.where(inside, OMEGA * diag / denom, 0.0)
-    inv_im = jnp.where(inside, -OMEGA * shift / denom, 0.0)
+    inverse = jnp.where(inside, OMEGA / (diag * diag + shift * shift), 0.0)
+    inv_re = diag * inverse
+    inv_im = -shift * inverse
 
     def damp(a, b):
         return a * inv_re - b * inv_im, a * inv_im + b * inv_re
@@ -291,8 +271,8 @@
         before = jnp.concatenate([nothing, v[:-1]], axis=0)
         return (
             (after, before),
-            (pltpu.roll(v, 15, axis=1), pltpu.roll(v, 1, axis=1)),
-            (pltpu.roll(v, wide - 1, axis=2), pltpu.roll(v, 1, axis=2)),
+            (pltpu.roll(v, rows - 1, axis=1), pltpu.roll(v, 1, axis=1)),
+            (pltpu.roll(v, cols - 1, axis=2), pltpu.roll(v, 1, axis=2)),
         )
 
     def helm(v, pairs):
@@ -319,10 +299,63 @@
     sa, sb = swept(re, im)
     ra, rb = remaining(re, sa), remaining(im, sb)
     ua, ub = swept(ra, rb)
-    res_ref[0] = ra[:, 0:8, 0:lo_n]
-    res_ref[1] = rb[:, 0:8, 0:lo_n]
-    sol_ref[0] = (sa + ua)[:, 0:8, 0:lo_n]
-    sol_ref[1] = (sb + ub)[:, 0:8, 0:lo_n]
+    return sa + ua, sb + ub, ra, rb
+
+
+def tile_of(c, t, r1_ref, perm_ref, wn_ref, halo_ref):
+    planes = perm_ref.shape[0] // 8
+    lanes = slice(t * 128, (t + 1) * 128)
+    if c < 3:
+        own = perm_ref[:, lanes] if c == 2 else r1_ref[c, :, lanes]
+    else:
+        own = wn_ref[c - 3, t]
+    return jnp.concatenate([own.reshape(planes, 8, 128), halo_ref[c, t].reshape(planes, 8, 128)], axis=1)
+
+
+def inner_kernel(r1_ref, perm_ref, wn_ref, halo_ref, sol_ref, res_ref):
+    tiles = halo_ref.shape[1]
+    fields = [
+        jnp.concatenate([tile_of(c, t, r1_ref, perm_ref, wn_ref, halo_ref) for t in range(tiles)], axis=2)
+        for c in range(7)
+    ]
+    sa, sb, ra, rb = iterate(*fields)
+    for k, (sol, res) in enumerate(((sa, ra), (sb, rb))):
+        sol_ref[k] = sol[:, 0:8, :]
+        res_ref[k] = res[:, 0:8, :]
+
+
+def final_kernel(
+    r1_ref, perm_ref, wn_ref, halo_ref, sol_in_ref, res_in_ref, pair_ref, other_ref, sol_ref, res_ref
+):
+    planes = perm_ref.shape[0] // 8
+    last = halo_ref.shape[1] - 1
+    lane = lax.broadcasted_iota(jnp.int32, (planes, 16, 128), 2)
+    even = lax.rem(lax.axis_index("gy"), 2) == 0
+    pair, other = pair_ref[...], other_ref[...]
+    from_right = jnp.where(even, pair, other)
+    from_left = jnp.where(even, other, pair)
+    fields = []
+    for c in range(7):
+        offset, width = COL_PLACE[c]
+        args = (r1_ref, perm_ref, wn_ref, halo_ref)
+        field = jnp.where(lane < 56, tile_of(c, 0, *args), 0.0)
+        field = jnp.where((lane >= 60) & (lane < 116), pltpu.roll(tile_of(c, last, *args), 116, axis=2), field)
+        field = jnp.where((lane >= 116) & (lane < 116 + width), pltpu.roll(from_right, 116 - offset, axis=2), field)
+        field = jnp.where(lane >= 128 - width, pltpu.roll(from_left, offset, axis=2), field)
+        fields.append(field)
+    sa, sb, ra, rb = iterate(*fields)
+    near = lane[:, 0:8, :]
+    for k, (sol, res) in enumerate(((sa, ra), (sb, rb))):
+        for out_ref, in_ref, value in ((sol_ref, sol_in_ref, sol), (res_ref, res_in_ref, res)):
+            value = value[:, 0:8, :]
+            for t in range(last + 1):
+                lanes = slice(t * 128, (t + 1) * 128)
+                tile = in_ref[k, :, :, lanes]
+                if t == 0:
+                    tile = jnp.where(near < 8, value, tile)
+                if t == last:
+                    tile = jnp.where(near >= 120, pltpu.roll(value, 12, axis=2), tile)
+                out_ref[k, :, :, lanes] = tile
 
 
 def in_vmem(n):
@@ -369,25 +402,19 @@
 
     tiles = cols // 128
 
-    def scatter_scratch(parts):
-        return [
-            pltpu.VMEM((slots, points), f32),
-            pltpu.VMEM((slots, points), f32),
-            pltpu.VMEM((parts, cols), f32),
-        ]
-
     def cost(parts):
         flops = 2 * parts * cols * slots * points
         return pl.CostEstimate(flops=flops, transcendentals=0, bytes_accessed=slots * CHANNELS * points * 4)
 
     strip = shape(13 * planes, cols)
     parts = 4 * cells + 14 * planes
-    r1, edges, pair, other = pl.pallas_call(
+    local = shape(slots, points)
+    r1, edges, pair, other, hi, lo = pl.pallas_call(
         first_kernel,
-        out_shape=(shape(2, cells, cols), shape(4, 2 * planes, cols), strip, strip),
+        out_shape=(shape(2, cells, cols), shape(4, 2 * planes, cols), strip, strip, local, local),
         in_specs=in_vmem(3),
-        out_specs=tuple(in_vmem(4)),
-        scratch_shapes=scatter_scratch(parts) + [pltpu.VMEM((3, tiles, cells, 128), f32)],
+        out_specs=tuple(in_vmem(6)),
+        scratch_shapes=[pltpu.VMEM((parts, cols), f32), pltpu.VMEM((3, tiles, cells, 128), f32)],
         compiler_params=params,
         cost_estimate=cost(parts),
         name="first",
@@ -398,13 +425,13 @@
     wn = pl.pallas_call(
         second_kernel,
         out_shape=shape(4, tiles, cells, 128),
-        in_specs=in_vmem(2),
+        in_specs=in_vmem(4),
         out_specs=in_vmem(1)[0],
-        scratch_shapes=scatter_scratch(parts),
+        scratch_shapes=[pltpu.VMEM((parts, cols), f32)],
         compiler_params=params,
         cost_estimate=cost(parts),
         name="second",
-    )(recv, edges)
+    )(recv, hi, lo, edges)
     pair, other, halo = pl.pallas_call(
         strip_kernel,
         out_shape=(shape(planes, 16, 128), shape(planes, 16, 128), shape(7, tiles, cells, 128)),
@@ -416,14 +443,23 @@
     from_pair = lax.ppermute(pair, "gy", [(i, i ^ 1) for i in range(gy)])
     from_other = lax.ppermute(other, "gy", [(i, (((i + 1) ^ 1) - 1) % gy) for i in range(gy)])
     field = shape(2, planes, rows, cols)
+    sol, res = pl.pallas_call(
+        inner_kernel,
+        out_shape=(field, field),
+        in_specs=in_vmem(4),
+        out_specs=tuple(in_vmem(2)),
+        compiler_params=params,
+        cost_estimate=cost(8 * planes),
+        name="inner",
+    )(r1, permittivity, wn, halo)
     return pl.pallas_call(
         final_kernel,
         out_shape=(field, field),
-        in_specs=in_vmem(6),
+        in_specs=in_vmem(8),
         out_specs=tuple(in_vmem(2)),
         compiler_params=params,
         name="final",
-    )(r1, permittivity, wn, halo, from_pair, from_other)
+    )(r1, permittivity, wn, halo, sol, res, from_pair, from_other)
 
 
 def solution(mesh):

time: 55 us -> 55 us (level)
    pallas_call x1 -> x2, Pallas kernels: 1.79 us -> 2.27 us  [the longest x1 1.53 us: per_device(): pl.pallas_call(final_kernel, out_shape=(field, field), in_specs=in_vmem(8...]
  transfers between devices with their start and end apart: 4 -> 4, of which waited for: 2 -> 2; matrix products, arithmetic and copies ran while one was open for 0% -> 0% of each run, Pallas kernels for 11% -> 12%
where the time goes in v2:
time: 55 us; the launch traced here: 54.9 us
  blocking collectives  27.4 us (50%)
  Pallas kernels  17.2 us (31%)
  starting transfers between devices  6.57 us (12%)
  waiting for transfers between devices  2.99 us (5%)
  between operations  0.71 us (1%)
    all_to_all x1, blocking collectives, per_device(): lax.all_to_all(send.reshape(-1), ('gx', 'gy'), split_axis=0, concat_axis=...  27.4 us
    pallas_call x1, Pallas kernels, per_device(): pl.pallas_call(first_kernel, out_shape=(shape(2, cells, cols), shape(4, 2...  7.08 us
    pallas_call x1, Pallas kernels, per_device(): pl.pallas_call(second_kernel, out_shape=shape(4, tiles, cells, 128), in_s...  5.85 us
    ppermute x1, starting transfers between devices, per_device(): lax.ppermute(other, 'gx', [(i, ((i + 1 ^ 1) - 1) % gx) for i in range(gx)])  3.08 us
    ppermute x1, waiting for transfers between devices, per_device(): lax.ppermute(other, 'gy', [(i, ((i + 1 ^ 1) - 1) % gy) for i in range(gy)])  2.66 us
    ppermute x1, starting transfers between devices, per_device(): from_pair = lax.ppermute(pair, 'gy', [(i, i ^ 1) for i in range(gy)])  2.23 us
    pallas_call x1, Pallas kernels, per_device(): pl.pallas_call(pack_kernel, out_shape=shape(slots * CHANNELS, points), in...  1.71 us
    pallas_call x1, Pallas kernels, per_device(): pl.pallas_call(final_kernel, out_shape=(field, field), in_specs=in_vmem(8...  1.53 us
  transfers between devices with their start and end apart: 4, of which 2 were waited for; matrix products, arithmetic and copies ran while one was open for 0% of the time, Pallas kernels for 12%

profile of v2, /device:TPU:1, one launch (start us, length us, event | category | flops | bytes accessed | tf_op | source)
XLA Modules:
  0.0 54.9 jit_solution(7908906507038797259)
XLA Ops:
  0.6 1.7 %pack.1 = f32[1536,128]{1,0:T(8,128)S(1)} custom-call(s32[128]{0:T(128)} %bitcast.13, f32[128,128]{1,0:T(8,128)} %dist_hbm.1, f32[3,128,128]{2,1,0:T(8,128)} %normal_hbm.1, f32[2,128,128]{2,1,0:T(8,128)} %inc_hbm.1, s32[128,128]{1,0:T(8,128)} %cell_hbm.1, s32[128,128]{1,0:T(8,128)} %mask_hbm.1), custom_call_target="tpu_custom_call" | custom-call | tf_op jit(solution)/shard_map/pack/pallas_call | solution.py:376
  2.3 0.0 copy-start
  2.4 0.0 copy-start.1
  2.4 27.4 %all_to_all.9 = f32[128,1536,1]{1,2,0:T(1,128)S(1)} all-to-all(f32[128,1536,1]{1,2,0:T(1,128)S(1)} %bitcast.5), channel_id=1, replica_groups=mesh['gx'=32,'gy'=4] {'gx','gy'}, dimensions={0} | all-to-all | bytes 1572864 | tf_op jit(solution)/shard_map/all_to_all | solution.py:397
  29.8 0.0 copy-done
  29.8 0.0 copy-done.1
  29.8 7.1 %first.1 = (f32[2,64,256]{2,1,0:T(8,128)S(1)}, f32[4,16,256]{2,1,0:T(8,128)S(1)}, f32[104,256]{1,0:T(8,128)S(1)}, f32[104,256]{1,0:T(8,128)S(1)}, f32[256,128]{1,0:T(8,128)S(1)}, /*index=5*/f32[256,128]{1,0:T(8,128)S(1)}) custom-call(f32[1536,128]{1,0:T(8,128)S(1)} %bitcast.6, f32[2,64,256]{2,1,0:T(8,128)S(1)} %bitcast.12, f32[64,256]{1,0:T(8,128)S(1)} %bitcast.8), custom_call_target="tpu_custom_call" | custom-call | flops 6174015488 | bytes 786432 | tf_op jit(solution)/shard_map/first/pallas_call | solution.py:412
  36.9 0.9 %collective-permute-start = (f32[104,256]{1,0:T(8,128)S(1)}, f32[104,256]{1,0:T(8,128)S(1)}, u32[]{:S(2)}, u32[]{:S(2)}) collective-permute-start(f32[104,256]{1,0:T(8,128)S(1)} %get-tuple-element.17), channel_id=1, source_target_pairs={{0,4},{4,0},{8,12},{12,8},{16,20},{20,16},{24,28},{28,24},{32,36},... | collective-permute-start | bytes 319496 | tf_op jit(solution)/shard_map/ppermute | solution.py:422
  37.8 3.1 %collective-permute-start.1 = (f32[104,256]{1,0:T(8,128)S(1)}, f32[104,256]{1,0:T(8,128)S(1)}, u32[]{:S(2)}, u32[]{:S(2)}) collective-permute-start(f32[104,256]{1,0:T(8,128)S(1)} %get-tuple-element.18), channel_id=1, source_target_pairs={{0,124},{4,8},{8,4},{12,16},{16,12},{20,24},{24,20},{28,32},{32,28... | collective-permute-start | bytes 319496 | tf_op jit(solution)/shard_map/ppermute | solution.py:423
  40.9 5.9 %second.1.wn_ref = f32[4,2,64,128]{3,2,1,0:T(8,128)S(1)} custom-call(f32[1536,128]{1,0:T(8,128)S(1)} %bitcast.7, f32[256,128]{1,0:T(8,128)S(1)} %get-tuple-element.14.hi_ref, f32[256,128]{1,0:T(8,128)S(1)} %get-tuple-element.15.lo_ref, f32[4,16,256]{2,1,0:T(8,128)S(1)} %get-tuple-element.16.edge_ref), custom_call_target="tpu_custom_call" | custom-call | flops 5637144576 | bytes 786432 | tf_op jit(solution)/shard_map/second/pallas_call | solution.py:425
  46.7 0.0 collective-permute-done.pair_ref
  46.7 0.3 collective-permute-done.1.other_ref
  47.1 0.3 strips.1
  47.3 2.2 %collective-permute-start.2 = (f32[8,16,128]{2,1,0:T(8,128)S(1)}, f32[8,16,128]{2,1,0:T(8,128)S(1)}, u32[]{:S(2)}, u32[]{:S(2)}) collective-permute-start(f32[8,16,128]{2,1,0:T(8,128)S(1)} %get-tuple-element.22), channel_id=1, source_target_pairs={{0,1},{1,0},{2,3},{3,2},{4,5},{5,4},{6,7},{7,6},{8,9},{9,8},{10,11... | collective-permute-start | bytes 196616 | tf_op jit(solution)/shard_map/ppermute | solution.py:443
  49.6 0.4 collective-permute-start.3
  49.9 0.7 %inner.1 = (f32[2,8,8,256]{3,2,1,0:T(8,128)S(1)}, f32[2,8,8,256]{3,2,1,0:T(8,128)S(1)}) custom-call(f32[2,64,256]{2,1,0:T(8,128)S(1)} %get-tuple-element.13.r1_ref, f32[64,256]{1,0:T(8,128)S(1)} %bitcast.10, f32[4,2,64,128]{3,2,1,0:T(8,128)S(1)} %second.1.wn_ref, f32[7,2,64,128]{3,2,1,0:T(8,128)S(1)} %get-tuple-element.19.halo_ref), custom_call_target="tpu_custom_call" | custom-call | flops 1073741824 | bytes 786432 | tf_op jit(solution)/shard_map/inner/pallas_call | solution.py:446
  50.7 0.0 collective-permute-done.2.pair_ref
  50.7 2.7 %collective-permute-done.3.other_ref = f32[8,16,128]{2,1,0:T(8,128)S(1)} collective-permute-done((f32[8,16,128]{2,1,0:T(8,128)S(1)}, f32[8,16,128]{2,1,0:T(8,128)S(1)}, u32[]{:S(2)}, u32[]{:S(2)}) %collective-permute-start.3) | collective-permute-done | bytes 65568 | tf_op jit(solution)/shard_map/ppermute | solution.py:444
  53.4 1.5 %final.1 = (f32[2,8,8,256]{3,2,1,0:T(8,128)}, f32[2,8,8,256]{3,2,1,0:T(8,128)}) custom-call(f32[2,64,256]{2,1,0:T(8,128)S(1)} %get-tuple-element.13.r1_ref, f32[64,256]{1,0:T(8,128)S(1)} %bitcast.11, f32[4,2,64,128]{3,2,1,0:T(8,128)S(1)} %second.1.wn_ref, f32[7,2,64,128]{3,2,1,0:T(8,128)S(1)} %get-tuple-element.19.halo_ref, ...), custom_call_target="tpu_custom_call" | custom-call | tf_op jit(solution)/shard_map/final/pallas_call | solution.py:455
Async XLA Ops:
  2.3 27.5 %copy-start = (f32[8,8,256]{2,1,0:T(8,128)S(1)}, f32[8,8,256]{2,1,0:T(8,128)}, u32[]{:S(2)}) copy-start(f32[8,8,256]{2,1,0:T(8,128)} %param.9) | copy-start | bytes 196612
  2.4 27.5 %copy-start.1 = (f32[2,8,8,256]{3,2,1,0:T(8,128)S(1)}, f32[2,8,8,256]{3,2,1,0:T(8,128)}, u32[]{:S(2)}) copy-start(f32[2,8,8,256]{3,2,1,0:T(8,128)} %param.8) | copy-start | bytes 393220
  36.9 9.8 %collective-permute-start = (f32[104,256]{1,0:T(8,128)S(1)}, f32[104,256]{1,0:T(8,128)S(1)}, u32[]{:S(2)}, u32[]{:S(2)}) collective-permute-start(f32[104,256]{1,0:T(8,128)S(1)} %get-tuple-element.17), channel_id=1, source_target_pairs={{0,4},{4,0},{8,12},{12,8},{16,20},{20,16},{24,28},{28,24},{32,36},... | collective-permute-start | bytes 319496 | tf_op jit(solution)/shard_map/ppermute | solution.py:422
  37.8 9.3 %collective-permute-start.1 = (f32[104,256]{1,0:T(8,128)S(1)}, f32[104,256]{1,0:T(8,128)S(1)}, u32[]{:S(2)}, u32[]{:S(2)}) collective-permute-start(f32[104,256]{1,0:T(8,128)S(1)} %get-tuple-element.18), channel_id=1, source_target_pairs={{0,124},{4,8},{8,4},{12,16},{16,12},{20,24},{24,20},{28,32},{32,28... | collective-permute-start | bytes 319496 | tf_op jit(solution)/shard_map/ppermute | solution.py:423
  47.3 3.4 %collective-permute-start.2 = (f32[8,16,128]{2,1,0:T(8,128)S(1)}, f32[8,16,128]{2,1,0:T(8,128)S(1)}, u32[]{:S(2)}, u32[]{:S(2)}) collective-permute-start(f32[8,16,128]{2,1,0:T(8,128)S(1)} %get-tuple-element.22), channel_id=1, source_target_pairs={{0,1},{1,0},{2,3},{3,2},{4,5},{5,4},{6,7},{7,6},{8,9},{9,8},{10,11... | collective-permute-start | bytes 196616 | tf_op jit(solution)/shard_map/ppermute | solution.py:443
  49.6 3.8 %collective-permute-start.3 = (f32[8,16,128]{2,1,0:T(8,128)S(1)}, f32[8,16,128]{2,1,0:T(8,128)S(1)}, u32[]{:S(2)}, u32[]{:S(2)}) collective-permute-start(f32[8,16,128]{2,1,0:T(8,128)S(1)} %get-tuple-element.23), channel_id=1, source_target_pairs={{0,3},{1,2},{2,1},{3,0},{4,7},{5,6},{6,5},{7,4},{8,11},{9,10},{10,... | collective-permute-start | bytes 196616 | tf_op jit(solution)/shard_map/ppermute | solution.py:444

commit v3 on v2

--- a/solution.py
+++ b/solution.py
@@ -22,15 +22,15 @@
 
 def pack_kernel(
     owner_hbm, dist_hbm, normal_hbm, inc_hbm, cell_hbm, mask_hbm, out_ref,
-    owner_ref, base_ref, count_ref, dist_ref, coef_ref, cell_ref, mask_ref, sems,
+    owner_ref, base_ref, count_ref, dist_ref, raw_ref, coef_ref, cell_ref, mask_ref, sems,
 ):
     blocks = dist_ref.shape[0]
     devices = count_ref.shape[0]
     copies = [
         pltpu.make_async_copy(owner_hbm, owner_ref, sems.at[0]),
         pltpu.make_async_copy(dist_hbm, dist_ref, sems.at[1]),
-        pltpu.make_async_copy(normal_hbm, coef_ref.at[pl.ds(0, 3)], sems.at[2]),
-        pltpu.make_async_copy(inc_hbm, coef_ref.at[pl.ds(3, 2)], sems.at[3]),
+        pltpu.make_async_copy(normal_hbm, raw_ref.at[pl.ds(0, 3)], sems.at[2]),
+        pltpu.make_async_copy(inc_hbm, raw_ref.at[pl.ds(3, 2)], sems.at[3]),
         pltpu.make_async_copy(cell_hbm, cell_ref, sems.at[4]),
         pltpu.make_async_copy(mask_hbm, mask_ref, sems.at[5]),
     ]
@@ -57,15 +57,14 @@
         copy.wait()
     half = 0.5 * TAU * dist_ref[...]
     for k in range(3):
-        coef_ref[k] = half * coef_ref[k]
+        rows = slice(k * blocks, (k + 1) * blocks)
+        coef_ref[rows] = half * raw_ref[k]
     for k in range(3, 5):
-        coef_ref[k] = TAU * coef_ref[k]
-    coef_ref[5] = jnp.where(mask_ref[...] > 0, cell_ref[...], 1 << 14).astype(f32)
+        coef_ref[k * blocks : (k + 1) * blocks] = TAU * raw_ref[k]
+    coef_ref[5 * blocks : 6 * blocks] = jnp.where(mask_ref[...] > 0, cell_ref[...], 1 << 14).astype(f32)
 
     def place(b, carry):
-        base = base_ref[b]
-        for c in range(CHANNELS):
-            out_ref[pl.ds(base + c, 1), :] = coef_ref[c, pl.ds(b, 1), :]
+        out_ref[pl.ds(base_ref[b], CHANNELS), :] = coef_ref[pl.ds(b, CHANNELS, stride=blocks), :]
         return carry
 
     lax.fori_loop(0, blocks, place, 0, unroll=8)
@@ -84,6 +83,7 @@
     slots = hi_ref.shape[0]
     lo_n = acc_ref.shape[1]
     per_step = min(GROUP, slots)
+    acc_ref[...] = jnp.zeros(acc_ref.shape, f32)
     one = jnp.ones((), bf16)
     zero = jnp.zeros((), bf16)
     targets = []
@@ -102,7 +102,7 @@
     def tall(tile, n):
         return jnp.concatenate([tile] * (n // 16), axis=0)
 
-    def step(g):
+    def step(g, carry):
         left, right = [], []
         for j in range(per_step):
             slot = g * per_step + j
@@ -121,16 +121,15 @@
                     pieces.append(jnp.where(hot, one, zero))
             left.append(jnp.concatenate(pieces, axis=0))
             right.append(jnp.where(lo_iota == tall(load(lo_ref, slot).astype(bf16), lo_n), one, zero))
-        total = lax.dot_general(
+        acc_ref[...] += lax.dot_general(
             jnp.concatenate(left, axis=1),
             jnp.concatenate(right, axis=1),
             (((1,), (1,)), ((), ())),
             preferred_element_type=f32,
         )
-        acc_ref[...] = total if g == 0 else acc_ref[...] + total
-
-    for g in range(slots // per_step):
-        step(g)
+        return carry
+
+    lax.fori_loop(0, slots // per_step, step, 0)
     sums, start = [], 0
     for rows, channels, count in groups:
         n = 8 * len(rows)
@@ -249,8 +248,15 @@
             moved = pltpu.roll(full, (sign * offset) % 128, axis=2)
             strip = jnp.where((place >= offset) & (place < offset + width), moved, strip)
         strips.append(jnp.where(position == edge, 0.0, strip))
-    out_pair_ref[...] = jnp.where(even, strips[1], strips[0])
-    out_other_ref[...] = jnp.where(even, strips[0], strips[1])
+    lane = lax.broadcasted_iota(jnp.int32, (16, 128), 1)
+    packed = []
+    for strip, base in zip(strips, (0, 112)):
+        flat = jnp.zeros((16, 128), f32)
+        for p in range(planes):
+            flat = jnp.where(lane >> 4 == p, pltpu.roll(strip[p], (16 * p - base) % 128, axis=1), flat)
+        packed.append(flat)
+    out_pair_ref[...] = jnp.where(even, packed[1], packed[0])
+    out_other_ref[...] = jnp.where(even, packed[0], packed[1])
 
 
 def iterate(re, im, perm, w, nz, nx, ny):
@@ -334,6 +340,8 @@
     pair, other = pair_ref[...], other_ref[...]
     from_right = jnp.where(even, pair, other)
     from_left = jnp.where(even, other, pair)
+    from_right = jnp.stack([pltpu.roll(from_right, (-16 * p) % 128, axis=1) for p in range(planes)])
+    from_left = jnp.stack([pltpu.roll(from_left, (112 - 16 * p) % 128, axis=1) for p in range(planes)])
     fields = []
     for c in range(7):
         offset, width = COL_PLACE[c]
@@ -383,7 +391,8 @@
             pltpu.SMEM((blocks,), jnp.int32),
             pltpu.SMEM((devices,), jnp.int32),
             pltpu.VMEM((blocks, points), f32),
-            pltpu.VMEM((CHANNELS, blocks, points), f32),
+            pltpu.VMEM((CHANNELS - 1, blocks, points), f32),
+            pltpu.VMEM((8 * blocks, points), f32),
             pltpu.VMEM((blocks, points), jnp.int32),
             pltpu.VMEM((blocks, points), jnp.int32),
             pltpu.SemaphoreType.DMA((6,)),
@@ -419,8 +428,8 @@
         cost_estimate=cost(parts),
         name="first",
     )(recv, rhs_field, permittivity)
+    from_other = lax.ppermute(other, "gx", [(i, (((i + 1) ^ 1) - 1) % gx) for i in range(gx)])
     from_pair = lax.ppermute(pair, "gx", [(i, i ^ 1) for i in range(gx)])
-    from_other = lax.ppermute(other, "gx", [(i, (((i + 1) ^ 1) - 1) % gx) for i in range(gx)])
     parts = 7 * 6 * planes
     wn = pl.pallas_call(
         second_kernel,
@@ -434,14 +443,14 @@
     )(recv, hi, lo, edges)
     pair, other, halo = pl.pallas_call(
         strip_kernel,
-        out_shape=(shape(planes, 16, 128), shape(planes, 16, 128), shape(7, tiles, cells, 128)),
+        out_shape=(shape(16, 128), shape(16, 128), shape(7, tiles, cells, 128)),
         in_specs=in_vmem(5),
         out_specs=tuple(in_vmem(3)),
         compiler_params=params,
         name="strips",
     )(r1, permittivity, wn, from_pair, from_other)
+    from_other = lax.ppermute(other, "gy", [(i, (((i + 1) ^ 1) - 1) % gy) for i in range(gy)])
     from_pair = lax.ppermute(pair, "gy", [(i, i ^ 1) for i in range(gy)])
-    from_other = lax.ppermute(other, "gy", [(i, (((i + 1) ^ 1) - 1) % gy) for i in range(gy)])
     field = shape(2, planes, rows, cols)
     sol, res = pl.pallas_call(
         inner_kernel,

time: 55 us -> 54.1 us (0.984)
  waiting for transfers between devices: 2.99 us -> 2 us
    ppermute x1, waiting for transfers between devices: 2.66 us -> 1.96 us  [per_device(): lax.ppermute(other, 'gy', [(i, ((i + 1 ^ 1) - 1) % gy) for i in range(gy)])]
  transfers between devices with their start and end apart: 4 -> 4, of which waited for: 2 -> 1; matrix products, arithmetic and copies ran while one was open for 0% -> 0% of each run, Pallas kernels for 12% -> 13%
where the time goes in v3:
time: 54.1 us; the launch traced here: 54 us
  blocking collectives  27.4 us (51%)
  Pallas kernels  17.2 us (32%)
  starting transfers between devices  6.56 us (12%)
  waiting for transfers between devices  2 us (4%)
  between operations  0.71 us (1%)
    all_to_all x1, blocking collectives, per_device(): lax.all_to_all(send.reshape(-1), ('gx', 'gy'), split_axis=0, concat_axis=...  27.4 us
    pallas_call x1, Pallas kernels, per_device(): pl.pallas_call(first_kernel, out_shape=(shape(2, cells, cols), shape(4, 2...  6.76 us
    pallas_call x1, Pallas kernels, per_device(): pl.pallas_call(second_kernel, out_shape=shape(4, tiles, cells, 128), in_s...  6.14 us
    ppermute x1, starting transfers between devices, per_device(): lax.ppermute(other, 'gx', [(i, ((i + 1 ^ 1) - 1) % gx) for i in range(gx)])  3.08 us
    ppermute x1, starting transfers between devices, per_device(): from_pair = lax.ppermute(pair, 'gy', [(i, i ^ 1) for i in range(gy)])  2.24 us
    ppermute x1, waiting for transfers between devices, per_device(): lax.ppermute(other, 'gy', [(i, ((i + 1 ^ 1) - 1) % gy) for i in range(gy)])  1.96 us
    pallas_call x1, Pallas kernels, per_device(): pl.pallas_call(pack_kernel, out_shape=shape(slots * CHANNELS, points), in...  1.7 us
    pallas_call x1, Pallas kernels, per_device(): pl.pallas_call(final_kernel, out_shape=(field, field), in_specs=in_vmem(8...  1.56 us
  transfers between devices with their start and end apart: 4, of which 1 were waited for; matrix products, arithmetic and copies ran while one was open for 0% of the time, Pallas kernels for 13%

profile of v3, /device:TPU:1, one launch (start us, length us, event | category | flops | bytes accessed | tf_op | source)
XLA Modules:
  0.0 54.0 jit_solution(2684737406351109484)
XLA Ops:
  0.6 1.7 %pack.1 = f32[1536,128]{1,0:T(8,128)S(1)} custom-call(s32[128]{0:T(128)} %bitcast.13, f32[128,128]{1,0:T(8,128)} %dist_hbm.1, f32[3,128,128]{2,1,0:T(8,128)} %normal_hbm.1, f32[2,128,128]{2,1,0:T(8,128)} %inc_hbm.1, s32[128,128]{1,0:T(8,128)} %cell_hbm.1, s32[128,128]{1,0:T(8,128)} %mask_hbm.1), custom_call_target="tpu_custom_call" | custom-call | tf_op jit(solution)/shard_map/pack/pallas_call | solution.py:384
  2.3 0.0 copy-start
  2.3 0.0 copy-start.1
  2.4 27.4 %all_to_all.9 = f32[128,1536,1]{1,2,0:T(1,128)S(1)} all-to-all(f32[128,1536,1]{1,2,0:T(1,128)S(1)} %bitcast.5), channel_id=1, replica_groups=mesh['gx'=32,'gy'=4] {'gx','gy'}, dimensions={0} | all-to-all | bytes 1572864 | tf_op jit(solution)/shard_map/all_to_all | solution.py:406
  29.8 0.0 copy-done
  29.8 0.0 copy-done.1
  29.8 6.8 %first.1 = (f32[2,64,256]{2,1,0:T(8,128)S(1)}, f32[4,16,256]{2,1,0:T(8,128)S(1)}, f32[104,256]{1,0:T(8,128)S(1)}, f32[104,256]{1,0:T(8,128)S(1)}, f32[256,128]{1,0:T(8,128)S(1)}, /*index=5*/f32[256,128]{1,0:T(8,128)S(1)}) custom-call(f32[1536,128]{1,0:T(8,128)S(1)} %bitcast.6, f32[2,64,256]{2,1,0:T(8,128)S(1)} %bitcast.12, f32[64,256]{1,0:T(8,128)S(1)} %bitcast.8), custom_call_target="tpu_custom_call" | custom-call | flops 6174015488 | bytes 786432 | tf_op jit(solution)/shard_map/first/pallas_call | solution.py:421
  36.6 0.9 %collective-permute-start = (f32[104,256]{1,0:T(8,128)S(1)}, f32[104,256]{1,0:T(8,128)S(1)}, u32[]{:S(2)}, u32[]{:S(2)}) collective-permute-start(f32[104,256]{1,0:T(8,128)S(1)} %get-tuple-element.17), channel_id=1, source_target_pairs={{0,4},{4,0},{8,12},{12,8},{16,20},{20,16},{24,28},{28,24},{32,36},... | collective-permute-start | bytes 319496 | tf_op jit(solution)/shard_map/ppermute | solution.py:432
  37.5 3.1 %collective-permute-start.1 = (f32[104,256]{1,0:T(8,128)S(1)}, f32[104,256]{1,0:T(8,128)S(1)}, u32[]{:S(2)}, u32[]{:S(2)}) collective-permute-start(f32[104,256]{1,0:T(8,128)S(1)} %get-tuple-element.18), channel_id=1, source_target_pairs={{0,124},{4,8},{8,4},{12,16},{16,12},{20,24},{24,20},{28,32},{32,28... | collective-permute-start | bytes 319496 | tf_op jit(solution)/shard_map/ppermute | solution.py:431
  40.5 6.1 %second.1.wn_ref = f32[4,2,64,128]{3,2,1,0:T(8,128)S(1)} custom-call(f32[1536,128]{1,0:T(8,128)S(1)} %bitcast.7, f32[256,128]{1,0:T(8,128)S(1)} %get-tuple-element.14.hi_ref, f32[256,128]{1,0:T(8,128)S(1)} %get-tuple-element.15.lo_ref, f32[4,16,256]{2,1,0:T(8,128)S(1)} %get-tuple-element.16.edge_ref), custom_call_target="tpu_custom_call" | custom-call | flops 5637144576 | bytes 786432 | tf_op jit(solution)/shard_map/second/pallas_call | solution.py:434
  46.7 0.0 collective-permute-done.pair_ref
  46.7 0.0 collective-permute-done.1.other_ref
  46.7 0.3 strips.1
  47.1 2.2 %collective-permute-start.2 = (f32[16,128]{1,0:T(8,128)S(1)}, f32[16,128]{1,0:T(8,128)S(1)}, u32[]{:S(2)}, u32[]{:S(2)}) collective-permute-start(f32[16,128]{1,0:T(8,128)S(1)} %get-tuple-element.22), channel_id=1, source_target_pairs={{0,1},{1,0},{2,3},{3,2},{4,5},{5,4},{6,7},{7,6},{8,9},{9,8},{10,11... | collective-permute-start | bytes 24584 | tf_op jit(solution)/shard_map/ppermute | solution.py:453
  49.3 0.4 collective-permute-start.3
  49.7 0.7 %inner.1 = (f32[2,8,8,256]{3,2,1,0:T(8,128)S(1)}, f32[2,8,8,256]{3,2,1,0:T(8,128)S(1)}) custom-call(f32[2,64,256]{2,1,0:T(8,128)S(1)} %get-tuple-element.13.r1_ref, f32[64,256]{1,0:T(8,128)S(1)} %bitcast.10, f32[4,2,64,128]{3,2,1,0:T(8,128)S(1)} %second.1.wn_ref, f32[7,2,64,128]{3,2,1,0:T(8,128)S(1)} %get-tuple-element.19.halo_ref), custom_call_target="tpu_custom_call" | custom-call | flops 1073741824 | bytes 786432 | tf_op jit(solution)/shard_map/inner/pallas_call | solution.py:455
  50.4 0.0 collective-permute-done.2.pair_ref
  50.4 2.0 %collective-permute-done.3.other_ref = f32[16,128]{1,0:T(8,128)S(1)} collective-permute-done((f32[16,128]{1,0:T(8,128)S(1)}, f32[16,128]{1,0:T(8,128)S(1)}, u32[]{:S(2)}, u32[]{:S(2)}) %collective-permute-start.3) | collective-permute-done | bytes 8224 | tf_op jit(solution)/shard_map/ppermute | solution.py:452
  52.4 1.6 %final.1 = (f32[2,8,8,256]{3,2,1,0:T(8,128)}, f32[2,8,8,256]{3,2,1,0:T(8,128)}) custom-call(f32[2,64,256]{2,1,0:T(8,128)S(1)} %get-tuple-element.13.r1_ref, f32[64,256]{1,0:T(8,128)S(1)} %bitcast.11, f32[4,2,64,128]{3,2,1,0:T(8,128)S(1)} %second.1.wn_ref, f32[7,2,64,128]{3,2,1,0:T(8,128)S(1)} %get-tuple-element.19.halo_ref, ...), custom_call_target="tpu_custom_call" | custom-call | tf_op jit(solution)/shard_map/final/pallas_call | solution.py:464
Async XLA Ops:
  2.3 27.5 %copy-start = (f32[8,8,256]{2,1,0:T(8,128)S(1)}, f32[8,8,256]{2,1,0:T(8,128)}, u32[]{:S(2)}) copy-start(f32[8,8,256]{2,1,0:T(8,128)} %param.9) | copy-start | bytes 196612
  2.3 27.5 %copy-start.1 = (f32[2,8,8,256]{3,2,1,0:T(8,128)S(1)}, f32[2,8,8,256]{3,2,1,0:T(8,128)}, u32[]{:S(2)}) copy-start(f32[2,8,8,256]{3,2,1,0:T(8,128)} %param.8) | copy-start | bytes 393220
  36.6 10.1 %collective-permute-start = (f32[104,256]{1,0:T(8,128)S(1)}, f32[104,256]{1,0:T(8,128)S(1)}, u32[]{:S(2)}, u32[]{:S(2)}) collective-permute-start(f32[104,256]{1,0:T(8,128)S(1)} %get-tuple-element.17), channel_id=1, source_target_pairs={{0,4},{4,0},{8,12},{12,8},{16,20},{20,16},{24,28},{28,24},{32,36},... | collective-permute-start | bytes 319496 | tf_op jit(solution)/shard_map/ppermute | solution.py:432
  37.5 9.3 %collective-permute-start.1 = (f32[104,256]{1,0:T(8,128)S(1)}, f32[104,256]{1,0:T(8,128)S(1)}, u32[]{:S(2)}, u32[]{:S(2)}) collective-permute-start(f32[104,256]{1,0:T(8,128)S(1)} %get-tuple-element.18), channel_id=1, source_target_pairs={{0,124},{4,8},{8,4},{12,16},{16,12},{20,24},{24,20},{28,32},{32,28... | collective-permute-start | bytes 319496 | tf_op jit(solution)/shard_map/ppermute | solution.py:431
  47.1 3.4 %collective-permute-start.2 = (f32[16,128]{1,0:T(8,128)S(1)}, f32[16,128]{1,0:T(8,128)S(1)}, u32[]{:S(2)}, u32[]{:S(2)}) collective-permute-start(f32[16,128]{1,0:T(8,128)S(1)} %get-tuple-element.22), channel_id=1, source_target_pairs={{0,1},{1,0},{2,3},{3,2},{4,5},{5,4},{6,7},{7,6},{8,9},{9,8},{10,11... | collective-permute-start | bytes 24584 | tf_op jit(solution)/shard_map/ppermute | solution.py:453
  49.3 3.1 %collective-permute-start.3 = (f32[16,128]{1,0:T(8,128)S(1)}, f32[16,128]{1,0:T(8,128)S(1)}, u32[]{:S(2)}, u32[]{:S(2)}) collective-permute-start(f32[16,128]{1,0:T(8,128)S(1)} %get-tuple-element.23), channel_id=1, source_target_pairs={{0,3},{1,2},{2,1},{3,0},{4,7},{5,6},{6,5},{7,4},{8,11},{9,10},{10,... | collective-permute-start | bytes 24584 | tf_op jit(solution)/shard_map/ppermute | solution.py:452

commit v4 on v3

--- a/solution.py
+++ b/solution.py
@@ -22,10 +22,9 @@
 
 def pack_kernel(
     owner_hbm, dist_hbm, normal_hbm, inc_hbm, cell_hbm, mask_hbm, out_ref,
-    owner_ref, base_ref, count_ref, dist_ref, raw_ref, coef_ref, cell_ref, mask_ref, sems,
+    owner_ref, first_ref, dist_ref, raw_ref, coef_ref, cell_ref, mask_ref, sems,
 ):
     blocks = dist_ref.shape[0]
-    devices = count_ref.shape[0]
     copies = [
         pltpu.make_async_copy(owner_hbm, owner_ref, sems.at[0]),
         pltpu.make_async_copy(dist_hbm, dist_ref, sems.at[1]),
@@ -38,21 +37,14 @@
         copy.start()
     out_ref[...] = jnp.full(out_ref.shape, -1.0, f32)
 
-    def clear(i, carry):
-        count_ref[i] = 0
+    copies[0].wait()
+
+    def note(i, carry):
+        b = blocks - 1 - i
+        first_ref[owner_ref[b]] = b
         return carry
 
-    lax.fori_loop(0, devices, clear, 0, unroll=8)
-    copies[0].wait()
-
-    def rank(b, carry):
-        owner = owner_ref[b]
-        seen = count_ref[owner]
-        count_ref[owner] = seen + 1
-        base_ref[b] = (owner * CAP + seen) * CHANNELS
-        return carry
-
-    lax.fori_loop(0, blocks, rank, 0, unroll=8)
+    lax.fori_loop(0, blocks, note, 0, unroll=16)
     for copy in copies[1:]:
         copy.wait()
     half = 0.5 * TAU * dist_ref[...]
@@ -64,7 +56,9 @@
     coef_ref[5 * blocks : 6 * blocks] = jnp.where(mask_ref[...] > 0, cell_ref[...], 1 << 14).astype(f32)
 
     def place(b, carry):
-        out_ref[pl.ds(base_ref[b], CHANNELS), :] = coef_ref[pl.ds(b, CHANNELS, stride=blocks), :]
+        owner = owner_ref[b]
+        base = (owner * CAP + jnp.where(first_ref[owner] == b, 0, 1)) * CHANNELS
+        out_ref[pl.ds(base, CHANNELS), :] = coef_ref[pl.ds(b, CHANNELS, stride=blocks), :]
         return carry
 
     lax.fori_loop(0, blocks, place, 0, unroll=8)
@@ -318,7 +312,8 @@
     return jnp.concatenate([own.reshape(planes, 8, 128), halo_ref[c, t].reshape(planes, 8, 128)], axis=1)
 
 
-def inner_kernel(r1_ref, perm_ref, wn_ref, halo_ref, sol_ref, res_ref):
+def inner_kernel(r1_ref, perm_ref, wn_ref, halo_ref, pair_ref, sol_ref, res_ref, pair_out_ref):
+    pair_out_ref[...] = pair_ref[...]
     tiles = halo_ref.shape[1]
     fields = [
         jnp.concatenate([tile_of(c, t, r1_ref, perm_ref, wn_ref, halo_ref) for t in range(tiles)], axis=2)
@@ -388,7 +383,6 @@
         out_specs=pl.BlockSpec(memory_space=pltpu.VMEM),
         scratch_shapes=[
             pltpu.SMEM((blocks,), jnp.int32),
-            pltpu.SMEM((blocks,), jnp.int32),
             pltpu.SMEM((devices,), jnp.int32),
             pltpu.VMEM((blocks, points), f32),
             pltpu.VMEM((CHANNELS - 1, blocks, points), f32),
@@ -450,17 +444,17 @@
         name="strips",
     )(r1, permittivity, wn, from_pair, from_other)
     from_other = lax.ppermute(other, "gy", [(i, (((i + 1) ^ 1) - 1) % gy) for i in range(gy)])
-    from_pair = lax.ppermute(pair, "gy", [(i, i ^ 1) for i in range(gy)])
     field = shape(2, planes, rows, cols)
-    sol, res = pl.pallas_call(
+    sol, res, pair = pl.pallas_call(
         inner_kernel,
-        out_shape=(field, field),
-        in_specs=in_vmem(4),
-        out_specs=tuple(in_vmem(2)),
+        out_shape=(field, field, shape(16, 128)),
+        in_specs=in_vmem(5),
+        out_specs=tuple(in_vmem(3)),
         compiler_params=params,
         cost_estimate=cost(8 * planes),
         name="inner",
-    )(r1, permittivity, wn, halo)
+    )(r1, permittivity, wn, halo, pair)
+    from_pair = lax.ppermute(pair, "gy", [(i, i ^ 1) for i in range(gy)])
     return pl.pallas_call(
         final_kernel,
         out_shape=(field, field),

time: 54.1 us -> 53.2 us (0.983)
  waiting for transfers between devices: 2 us -> 1.21 us
    ppermute x1, starting transfers between devices: 2.24 us -> 0.09 us  [per_device(): from_pair = lax.ppermute(pair, 'gy', [(i, i ^ 1) for i in range(gy)])]
    ppermute x1, starting transfers between devices: 0.37 us -> 2.51 us  [per_device(): lax.ppermute(other, 'gy', [(i, ((i + 1 ^ 1) - 1) % gy) for i in range(gy)])]
    ppermute x1, waiting for transfers between devices: 1.96 us -> 0.49 us  [per_device(): lax.ppermute(other, 'gy', [(i, ((i + 1 ^ 1) - 1) % gy) for i in range(gy)])]
    ppermute x1, waiting for transfers between devices: 0.01 us -> 0.67 us  [per_device(): from_pair = lax.ppermute(pair, 'gy', [(i, i ^ 1) for i in range(gy)])]
  transfers between devices with their start and end apart: 4 -> 4, of which waited for: 1 -> 2; matrix products, arithmetic and copies ran while one was open for 0% -> 0% of each run, Pallas kernels for 13% -> 13%
where the time goes in v4:
time: 53.2 us; the launch traced here: 53.1 us
  blocking collectives  27.4 us (52%)
  Pallas kernels  17.1 us (32%)
  starting transfers between devices  6.56 us (12%)
  waiting for transfers between devices  1.21 us (2%)
  between operations  0.71 us (1%)
    all_to_all x1, blocking collectives, per_device(): lax.all_to_all(send.reshape(-1), ('gx', 'gy'), split_axis=0, concat_axis=...  27.4 us
    pallas_call x1, Pallas kernels, per_device(): pl.pallas_call(first_kernel, out_shape=(shape(2, cells, cols), shape(4, 2...  6.76 us
    pallas_call x1, Pallas kernels, per_device(): pl.pallas_call(second_kernel, out_shape=shape(4, tiles, cells, 128), in_s...  6.13 us
    ppermute x1, starting transfers between devices, per_device(): lax.ppermute(other, 'gx', [(i, ((i + 1 ^ 1) - 1) % gx) for i in range(gx)])  3.08 us
    ppermute x1, starting transfers between devices, per_device(): lax.ppermute(other, 'gy', [(i, ((i + 1 ^ 1) - 1) % gy) for i in range(gy)])  2.51 us
    pallas_call x1, Pallas kernels, per_device(): pl.pallas_call(pack_kernel, out_shape=shape(slots * CHANNELS, points), in...  1.62 us
    pallas_call x1, Pallas kernels, per_device(): pl.pallas_call(final_kernel, out_shape=(field, field), in_specs=in_vmem(8...  1.56 us
  transfers between devices with their start and end apart: 4, of which 2 were waited for; matrix products, arithmetic and copies ran while one was open for 0% of the time, Pallas kernels for 13%

profile of v4, /device:TPU:1, one launch (start us, length us, event | category | flops | bytes accessed | tf_op | source)
XLA Modules:
  0.0 53.1 jit_solution(1938417651956636144)
XLA Ops:
  0.6 1.6 %pack.1 = f32[1536,128]{1,0:T(8,128)S(1)} custom-call(s32[128]{0:T(128)} %bitcast.13, f32[128,128]{1,0:T(8,128)} %dist_hbm.1, f32[3,128,128]{2,1,0:T(8,128)} %normal_hbm.1, f32[2,128,128]{2,1,0:T(8,128)} %inc_hbm.1, s32[128,128]{1,0:T(8,128)} %cell_hbm.1, s32[128,128]{1,0:T(8,128)} %mask_hbm.1), custom_call_target="tpu_custom_call" | custom-call | tf_op jit(solution)/shard_map/pack/pallas_call | solution.py:379
  2.3 0.0 copy-start
  2.3 0.0 copy-start.1
  2.3 27.4 %all_to_all.9 = f32[128,1536,1]{1,2,0:T(1,128)S(1)} all-to-all(f32[128,1536,1]{1,2,0:T(1,128)S(1)} %bitcast.5), channel_id=1, replica_groups=mesh['gx'=32,'gy'=4] {'gx','gy'}, dimensions={0} | all-to-all | bytes 1572864 | tf_op jit(solution)/shard_map/all_to_all | solution.py:400
  29.7 0.0 copy-done
  29.7 0.0 copy-done.1
  29.7 6.8 %first.1 = (f32[2,64,256]{2,1,0:T(8,128)S(1)}, f32[4,16,256]{2,1,0:T(8,128)S(1)}, f32[104,256]{1,0:T(8,128)S(1)}, f32[104,256]{1,0:T(8,128)S(1)}, f32[256,128]{1,0:T(8,128)S(1)}, /*index=5*/f32[256,128]{1,0:T(8,128)S(1)}) custom-call(f32[1536,128]{1,0:T(8,128)S(1)} %bitcast.6, f32[2,64,256]{2,1,0:T(8,128)S(1)} %bitcast.12, f32[64,256]{1,0:T(8,128)S(1)} %bitcast.8), custom_call_target="tpu_custom_call" | custom-call | flops 6174015488 | bytes 786432 | tf_op jit(solution)/shard_map/first/pallas_call | solution.py:415
  36.5 0.9 %collective-permute-start = (f32[104,256]{1,0:T(8,128)S(1)}, f32[104,256]{1,0:T(8,128)S(1)}, u32[]{:S(2)}, u32[]{:S(2)}) collective-permute-start(f32[104,256]{1,0:T(8,128)S(1)} %get-tuple-element.18), channel_id=1, source_target_pairs={{0,4},{4,0},{8,12},{12,8},{16,20},{20,16},{24,28},{28,24},{32,36},... | collective-permute-start | bytes 319496 | tf_op jit(solution)/shard_map/ppermute | solution.py:426
  37.4 3.1 %collective-permute-start.1 = (f32[104,256]{1,0:T(8,128)S(1)}, f32[104,256]{1,0:T(8,128)S(1)}, u32[]{:S(2)}, u32[]{:S(2)}) collective-permute-start(f32[104,256]{1,0:T(8,128)S(1)} %get-tuple-element.19), channel_id=1, source_target_pairs={{0,124},{4,8},{8,4},{12,16},{16,12},{20,24},{24,20},{28,32},{32,28... | collective-permute-start | bytes 319496 | tf_op jit(solution)/shard_map/ppermute | solution.py:425
  40.5 6.1 %second.1.wn_ref = f32[4,2,64,128]{3,2,1,0:T(8,128)S(1)} custom-call(f32[1536,128]{1,0:T(8,128)S(1)} %bitcast.7, f32[256,128]{1,0:T(8,128)S(1)} %get-tuple-element.15.hi_ref, f32[256,128]{1,0:T(8,128)S(1)} %get-tuple-element.16.lo_ref, f32[4,16,256]{2,1,0:T(8,128)S(1)} %get-tuple-element.17.edge_ref), custom_call_target="tpu_custom_call" | custom-call | flops 5637144576 | bytes 786432 | tf_op jit(solution)/shard_map/second/pallas_call | solution.py:428
  46.6 0.0 collective-permute-done.pair_ref
  46.6 0.0 collective-permute-done.1.other_ref
  46.7 0.3 strips.1
  47.0 2.5 %collective-permute-start.3 = (f32[16,128]{1,0:T(8,128)S(1)}, f32[16,128]{1,0:T(8,128)S(1)}, u32[]{:S(2)}, u32[]{:S(2)}) collective-permute-start(f32[16,128]{1,0:T(8,128)S(1)} %get-tuple-element.25), channel_id=1, source_target_pairs={{0,3},{1,2},{2,1},{3,0},{4,7},{5,6},{6,5},{7,4},{8,11},{9,10},{10,... | collective-permute-start | bytes 24584 | tf_op jit(solution)/shard_map/ppermute | solution.py:446
  49.5 0.7 %inner.1 = (f32[2,8,8,256]{3,2,1,0:T(8,128)S(1)}, f32[2,8,8,256]{3,2,1,0:T(8,128)S(1)}, f32[16,128]{1,0:T(8,128)S(1)}) custom-call(f32[2,64,256]{2,1,0:T(8,128)S(1)} %get-tuple-element.14.r1_ref, f32[64,256]{1,0:T(8,128)S(1)} %bitcast.10, f32[4,2,64,128]{3,2,1,0:T(8,128)S(1)} %second.1.wn_ref, f32[7,2,64,128]{3,2,1,0:T(8,128)S(1)} %get-tuple-element.20.halo_ref, ...), custom_call_target="tpu_custom_call" | custom-call | flops 1073741824 | bytes 786432 | tf_op jit(solution)/shard_map/inner/pallas_call | solution.py:448
  50.3 0.1 collective-permute-start.2
  50.4 0.5 collective-permute-done.3.other_ref
  50.8 0.7 %collective-permute-done.2.pair_ref = f32[16,128]{1,0:T(8,128)S(1)} collective-permute-done((f32[16,128]{1,0:T(8,128)S(1)}, f32[16,128]{1,0:T(8,128)S(1)}, u32[]{:S(2)}, u32[]{:S(2)}) %collective-permute-start.2) | collective-permute-done | bytes 8224 | tf_op jit(solution)/shard_map/ppermute | solution.py:457
  51.5 1.6 %final.1 = (f32[2,8,8,256]{3,2,1,0:T(8,128)}, f32[2,8,8,256]{3,2,1,0:T(8,128)}) custom-call(f32[2,64,256]{2,1,0:T(8,128)S(1)} %get-tuple-element.14.r1_ref, f32[64,256]{1,0:T(8,128)S(1)} %bitcast.11, f32[4,2,64,128]{3,2,1,0:T(8,128)S(1)} %second.1.wn_ref, f32[7,2,64,128]{3,2,1,0:T(8,128)S(1)} %get-tuple-element.20.halo_ref, ...), custom_call_target="tpu_custom_call" | custom-call | tf_op jit(solution)/shard_map/final/pallas_call | solution.py:458
Async XLA Ops:
  2.3 27.5 %copy-start = (f32[8,8,256]{2,1,0:T(8,128)S(1)}, f32[8,8,256]{2,1,0:T(8,128)}, u32[]{:S(2)}) copy-start(f32[8,8,256]{2,1,0:T(8,128)} %param.9) | copy-start | bytes 196612
  2.3 27.5 %copy-start.1 = (f32[2,8,8,256]{3,2,1,0:T(8,128)S(1)}, f32[2,8,8,256]{3,2,1,0:T(8,128)}, u32[]{:S(2)}) copy-start(f32[2,8,8,256]{3,2,1,0:T(8,128)} %param.8) | copy-start | bytes 393220
  36.5 10.1 %collective-permute-start = (f32[104,256]{1,0:T(8,128)S(1)}, f32[104,256]{1,0:T(8,128)S(1)}, u32[]{:S(2)}, u32[]{:S(2)}) collective-permute-start(f32[104,256]{1,0:T(8,128)S(1)} %get-tuple-element.18), channel_id=1, source_target_pairs={{0,4},{4,0},{8,12},{12,8},{16,20},{20,16},{24,28},{28,24},{32,36},... | collective-permute-start | bytes 319496 | tf_op jit(solution)/shard_map/ppermute | solution.py:426
  37.4 9.3 %collective-permute-start.1 = (f32[104,256]{1,0:T(8,128)S(1)}, f32[104,256]{1,0:T(8,128)S(1)}, u32[]{:S(2)}, u32[]{:S(2)}) collective-permute-start(f32[104,256]{1,0:T(8,128)S(1)} %get-tuple-element.19), channel_id=1, source_target_pairs={{0,124},{4,8},{8,4},{12,16},{16,12},{20,24},{24,20},{28,32},{32,28... | collective-permute-start | bytes 319496 | tf_op jit(solution)/shard_map/ppermute | solution.py:425
  47.0 3.9 %collective-permute-start.3 = (f32[16,128]{1,0:T(8,128)S(1)}, f32[16,128]{1,0:T(8,128)S(1)}, u32[]{:S(2)}, u32[]{:S(2)}) collective-permute-start(f32[16,128]{1,0:T(8,128)S(1)} %get-tuple-element.25), channel_id=1, source_target_pairs={{0,3},{1,2},{2,1},{3,0},{4,7},{5,6},{6,5},{7,4},{8,11},{9,10},{10,... | collective-permute-start | bytes 24584 | tf_op jit(solution)/shard_map/ppermute | solution.py:446
  50.3 1.3 %collective-permute-start.2 = (f32[16,128]{1,0:T(8,128)S(1)}, f32[16,128]{1,0:T(8,128)S(1)}, u32[]{:S(2)}, u32[]{:S(2)}) collective-permute-start(f32[16,128]{1,0:T(8,128)S(1)} %get-tuple-element.24), channel_id=1, source_target_pairs={{0,1},{1,0},{2,3},{3,2},{4,5},{5,4},{6,7},{7,6},{8,9},{9,8},{10,11... | collective-permute-start | bytes 24584 | tf_op jit(solution)/shard_map/ppermute | solution.py:457

commit v5 on v4

--- a/solution.py
+++ b/solution.py
@@ -25,6 +25,7 @@
     owner_ref, first_ref, dist_ref, raw_ref, coef_ref, cell_ref, mask_ref, sems,
 ):
     blocks = dist_ref.shape[0]
+    devices = first_ref.shape[0]
     copies = [
         pltpu.make_async_copy(owner_hbm, owner_ref, sems.at[0]),
         pltpu.make_async_copy(dist_hbm, dist_ref, sems.at[1]),
@@ -57,11 +58,12 @@
 
     def place(b, carry):
         owner = owner_ref[b]
-        base = (owner * CAP + jnp.where(first_ref[owner] == b, 0, 1)) * CHANNELS
+        peer = (owner & 1) * (devices // 2) + (owner >> 1)
+        base = (peer * CAP + jnp.where(first_ref[owner] == b, 0, 1)) * CHANNELS
         out_ref[pl.ds(base, CHANNELS), :] = coef_ref[pl.ds(b, CHANNELS, stride=blocks), :]
         return carry
 
-    lax.fori_loop(0, blocks, place, 0, unroll=8)
+    lax.fori_loop(0, blocks, place, 0, unroll=16)
 
 
 def split_cells(recv_ref, hi_ref, lo_ref):
@@ -397,7 +399,10 @@
         pltpu.with_memory_space_constraint(x, pltpu.HBM)
         for x in (surf_owner[:, 0], surf_dist, surf_normal, surf_inc, surf_cell, surf_mask)
     ])
-    recv = lax.all_to_all(send.reshape(-1), ("gx", "gy"), split_axis=0, concat_axis=0, tiled=True)
+    peers = list(range(0, devices, 2)) + list(range(1, devices, 2))
+    recv = lax.all_to_all(
+        send.reshape(-1), ("gx", "gy"), split_axis=0, concat_axis=0, tiled=True, axis_index_groups=[peers]
+    )
     recv = recv.reshape(slots * CHANNELS, points)
     cells = planes * rows
     rhs_field = rhs_field.reshape(2, cells, cols)

time: 53.2 us -> 52.9 us (level)
  blocking collectives: 27.4 us -> 26.8 us
    ppermute x1, starting transfers between devices: 0.88 us -> 1.64 us  [per_device(): from_pair = lax.ppermute(pair, 'gx', [(i, i ^ 1) for i in range(gx)])]
    ppermute x1, starting transfers between devices: 2.51 us -> 1.86 us  [per_device(): lax.ppermute(other, 'gy', [(i, ((i + 1 ^ 1) - 1) % gy) for i in range(gy)])]
    all_to_all x1, blocking collectives: 27.4 us -> 26.8 us  [per_device(): lax.all_to_all(send.reshape(-1), ('gx', 'gy'), split_axis=0, concat_axis=...]
  transfers between devices with their start and end apart: 4 -> 4, of which waited for: 2 -> 3; matrix products, arithmetic and copies ran while one was open for 0% -> 0% of each run, Pallas kernels for 13% -> 13%
where the time goes in v5:
time: 52.9 us; the launch traced here: 52.7 us
  blocking collectives  26.8 us (51%)
  Pallas kernels  17.2 us (33%)
  starting transfers between devices  6.63 us (13%)
  waiting for transfers between devices  1.32 us (2%)
  between operations  0.7 us (1%)
    all_to_all x1, blocking collectives, per_device(): lax.all_to_all(send.reshape(-1), ('gx', 'gy'), split_axis=0, concat_axis=...  26.8 us
    pallas_call x1, Pallas kernels, per_device(): pl.pallas_call(first_kernel, out_shape=(shape(2, cells, cols), shape(4, 2...  6.76 us
    pallas_call x1, Pallas kernels, per_device(): pl.pallas_call(second_kernel, out_shape=shape(4, tiles, cells, 128), in_s...  6.14 us
    ppermute x1, starting transfers between devices, per_device(): lax.ppermute(other, 'gx', [(i, ((i + 1 ^ 1) - 1) % gx) for i in range(gx)])  2.63 us
    ppermute x1, starting transfers between devices, per_device(): lax.ppermute(other, 'gy', [(i, ((i + 1 ^ 1) - 1) % gy) for i in range(gy)])  1.86 us
    pallas_call x1, Pallas kernels, per_device(): pl.pallas_call(pack_kernel, out_shape=shape(slots * CHANNELS, points), in...  1.68 us
    ppermute x1, starting transfers between devices, per_device(): from_pair = lax.ppermute(pair, 'gx', [(i, i ^ 1) for i in range(gx)])  1.64 us
    pallas_call x1, Pallas kernels, per_device(): pl.pallas_call(final_kernel, out_shape=(field, field), in_specs=in_vmem(8...  1.56 us
  transfers between devices with their start and end apart: 4, of which 3 were waited for; matrix products, arithmetic and copies ran while one was open for 0% of the time, Pallas kernels for 13%

profile of v5, /device:TPU:1, one launch (start us, length us, event | category | flops | bytes accessed | tf_op | source)
XLA Modules:
  0.0 52.7 jit_solution(18359540558716959208)
XLA Ops:
  0.6 1.7 %pack.1 = f32[1536,128]{1,0:T(8,128)S(1)} custom-call(s32[128]{0:T(128)} %bitcast.13, f32[128,128]{1,0:T(8,128)} %dist_hbm.1, f32[3,128,128]{2,1,0:T(8,128)} %normal_hbm.1, f32[2,128,128]{2,1,0:T(8,128)} %inc_hbm.1, s32[128,128]{1,0:T(8,128)} %cell_hbm.1, s32[128,128]{1,0:T(8,128)} %mask_hbm.1), custom_call_target="tpu_custom_call" | custom-call | tf_op jit(solution)/shard_map/pack/pallas_call | solution.py:381
  2.3 0.0 copy-start
  2.3 0.0 copy-start.1
  2.3 26.8 %all_to_all.9 = f32[128,1536,1]{1,2,0:T(1,128)S(1)} all-to-all(f32[128,1536,1]{1,2,0:T(1,128)S(1)} %bitcast.5), channel_id=1, replica_groups={{0,2,4,6,8,10,12,14,16,18,20,22,24,26,28,30,32,34,36,38,40,42,44,46,48,..., dimensions={0} | all-to-all | bytes 1572864 | tf_op jit(solution)/shard_map/all_to_all | solution.py:403
  29.2 0.0 copy-done
  29.2 0.0 copy-done.1
  29.2 6.8 %first.1 = (f32[2,64,256]{2,1,0:T(8,128)S(1)}, f32[4,16,256]{2,1,0:T(8,128)S(1)}, f32[104,256]{1,0:T(8,128)S(1)}, f32[104,256]{1,0:T(8,128)S(1)}, f32[256,128]{1,0:T(8,128)S(1)}, /*index=5*/f32[256,128]{1,0:T(8,128)S(1)}) custom-call(f32[1536,128]{1,0:T(8,128)S(1)} %bitcast.6, f32[2,64,256]{2,1,0:T(8,128)S(1)} %bitcast.12, f32[64,256]{1,0:T(8,128)S(1)} %bitcast.8), custom_call_target="tpu_custom_call" | custom-call | flops 6174015488 | bytes 786432 | tf_op jit(solution)/shard_map/first/pallas_call | solution.py:420
  36.0 1.6 %collective-permute-start = (f32[104,256]{1,0:T(8,128)S(1)}, f32[104,256]{1,0:T(8,128)S(1)}, u32[]{:S(2)}, u32[]{:S(2)}) collective-permute-start(f32[104,256]{1,0:T(8,128)S(1)} %get-tuple-element.18), channel_id=1, source_target_pairs={{0,4},{4,0},{8,12},{12,8},{16,20},{20,16},{24,28},{28,24},{32,36},... | collective-permute-start | bytes 319496 | tf_op jit(solution)/shard_map/ppermute | solution.py:431
  37.6 2.6 %collective-permute-start.1 = (f32[104,256]{1,0:T(8,128)S(1)}, f32[104,256]{1,0:T(8,128)S(1)}, u32[]{:S(2)}, u32[]{:S(2)}) collective-permute-start(f32[104,256]{1,0:T(8,128)S(1)} %get-tuple-element.19), channel_id=1, source_target_pairs={{0,124},{4,8},{8,4},{12,16},{16,12},{20,24},{24,20},{28,32},{32,28... | collective-permute-start | bytes 319496 | tf_op jit(solution)/shard_map/ppermute | solution.py:430
  40.2 6.1 %second.1.wn_ref = f32[4,2,64,128]{3,2,1,0:T(8,128)S(1)} custom-call(f32[1536,128]{1,0:T(8,128)S(1)} %bitcast.7, f32[256,128]{1,0:T(8,128)S(1)} %get-tuple-element.15.hi_ref, f32[256,128]{1,0:T(8,128)S(1)} %get-tuple-element.16.lo_ref, f32[4,16,256]{2,1,0:T(8,128)S(1)} %get-tuple-element.17.edge_ref), custom_call_target="tpu_custom_call" | custom-call | flops 5637144576 | bytes 786432 | tf_op jit(solution)/shard_map/second/pallas_call | solution.py:433
  46.4 0.0 collective-permute-done.pair_ref
  46.4 0.5 collective-permute-done.1.other_ref
  46.9 0.3 strips.1
  47.2 1.9 %collective-permute-start.3 = (f32[16,128]{1,0:T(8,128)S(1)}, f32[16,128]{1,0:T(8,128)S(1)}, u32[]{:S(2)}, u32[]{:S(2)}) collective-permute-start(f32[16,128]{1,0:T(8,128)S(1)} %get-tuple-element.25), channel_id=1, source_target_pairs={{0,3},{1,2},{2,1},{3,0},{4,7},{5,6},{6,5},{7,4},{8,11},{9,10},{10,... | collective-permute-start | bytes 24584 | tf_op jit(solution)/shard_map/ppermute | solution.py:451
  49.1 0.7 %inner.1 = (f32[2,8,8,256]{3,2,1,0:T(8,128)S(1)}, f32[2,8,8,256]{3,2,1,0:T(8,128)S(1)}, f32[16,128]{1,0:T(8,128)S(1)}) custom-call(f32[2,64,256]{2,1,0:T(8,128)S(1)} %get-tuple-element.14.r1_ref, f32[64,256]{1,0:T(8,128)S(1)} %bitcast.10, f32[4,2,64,128]{3,2,1,0:T(8,128)S(1)} %second.1.wn_ref, f32[7,2,64,128]{3,2,1,0:T(8,128)S(1)} %get-tuple-element.20.halo_ref, ...), custom_call_target="tpu_custom_call" | custom-call | flops 1073741824 | bytes 786432 | tf_op jit(solution)/shard_map/inner/pallas_call | solution.py:453
  49.8 0.5 collective-permute-start.2
  50.3 0.1 collective-permute-done.3.other_ref
  50.4 0.8 %collective-permute-done.2.pair_ref = f32[16,128]{1,0:T(8,128)S(1)} collective-permute-done((f32[16,128]{1,0:T(8,128)S(1)}, f32[16,128]{1,0:T(8,128)S(1)}, u32[]{:S(2)}, u32[]{:S(2)}) %collective-permute-start.2) | collective-permute-done | bytes 8224 | tf_op jit(solution)/shard_map/ppermute | solution.py:462
  51.2 1.6 %final.1 = (f32[2,8,8,256]{3,2,1,0:T(8,128)}, f32[2,8,8,256]{3,2,1,0:T(8,128)}) custom-call(f32[2,64,256]{2,1,0:T(8,128)S(1)} %get-tuple-element.14.r1_ref, f32[64,256]{1,0:T(8,128)S(1)} %bitcast.11, f32[4,2,64,128]{3,2,1,0:T(8,128)S(1)} %second.1.wn_ref, f32[7,2,64,128]{3,2,1,0:T(8,128)S(1)} %get-tuple-element.20.halo_ref, ...), custom_call_target="tpu_custom_call" | custom-call | tf_op jit(solution)/shard_map/final/pallas_call | solution.py:463
Async XLA Ops:
  2.3 26.9 %copy-start = (f32[8,8,256]{2,1,0:T(8,128)S(1)}, f32[8,8,256]{2,1,0:T(8,128)}, u32[]{:S(2)}) copy-start(f32[8,8,256]{2,1,0:T(8,128)} %param.9) | copy-start | bytes 196612
  2.3 26.9 %copy-start.1 = (f32[2,8,8,256]{3,2,1,0:T(8,128)S(1)}, f32[2,8,8,256]{3,2,1,0:T(8,128)}, u32[]{:S(2)}) copy-start(f32[2,8,8,256]{3,2,1,0:T(8,128)} %param.8) | copy-start | bytes 393220
  36.0 10.4 %collective-permute-start = (f32[104,256]{1,0:T(8,128)S(1)}, f32[104,256]{1,0:T(8,128)S(1)}, u32[]{:S(2)}, u32[]{:S(2)}) collective-permute-start(f32[104,256]{1,0:T(8,128)S(1)} %get-tuple-element.18), channel_id=1, source_target_pairs={{0,4},{4,0},{8,12},{12,8},{16,20},{20,16},{24,28},{28,24},{32,36},... | collective-permute-start | bytes 319496 | tf_op jit(solution)/shard_map/ppermute | solution.py:431
  37.6 9.3 %collective-permute-start.1 = (f32[104,256]{1,0:T(8,128)S(1)}, f32[104,256]{1,0:T(8,128)S(1)}, u32[]{:S(2)}, u32[]{:S(2)}) collective-permute-start(f32[104,256]{1,0:T(8,128)S(1)} %get-tuple-element.19), channel_id=1, source_target_pairs={{0,124},{4,8},{8,4},{12,16},{16,12},{20,24},{24,20},{28,32},{32,28... | collective-permute-start | bytes 319496 | tf_op jit(solution)/shard_map/ppermute | solution.py:430
  47.2 3.2 %collective-permute-start.3 = (f32[16,128]{1,0:T(8,128)S(1)}, f32[16,128]{1,0:T(8,128)S(1)}, u32[]{:S(2)}, u32[]{:S(2)}) collective-permute-start(f32[16,128]{1,0:T(8,128)S(1)} %get-tuple-element.25), channel_id=1, source_target_pairs={{0,3},{1,2},{2,1},{3,0},{4,7},{5,6},{6,5},{7,4},{8,11},{9,10},{10,... | collective-permute-start | bytes 24584 | tf_op jit(solution)/shard_map/ppermute | solution.py:451
  49.8 1.3 %collective-permute-start.2 = (f32[16,128]{1,0:T(8,128)S(1)}, f32[16,128]{1,0:T(8,128)S(1)}, u32[]{:S(2)}, u32[]{:S(2)}) collective-permute-start(f32[16,128]{1,0:T(8,128)S(1)} %get-tuple-element.24), channel_id=1, source_target_pairs={{0,1},{1,0},{2,3},{3,2},{4,5},{5,4},{6,7},{7,6},{8,9},{9,8},{10,11... | collective-permute-start | bytes 24584 | tf_op jit(solution)/shard_map/ppermute | solution.py:462

commit v6 on v4

--- a/solution.py
+++ b/solution.py
@@ -152,26 +152,30 @@
         ref[k, t, pl.ds(row, ref.shape[2] // 8, stride=8), :] = value[:, t * 128 : (t + 1) * 128]
 
 
-ALL = tuple(range(8))
+OUTER = (0, 1, 2, 5, 6, 7)
+MIDDLE = (3, 4)
 EDGES = (0, 7)
 INNER = (1, 2, 3, 4, 5, 6)
 FIELDS = ((0, 1, 2), True)
 
 
+def subtract_rows(tile_ref, k, rows, sums):
+    planes = tile_ref.shape[2] // 8
+    for j, r in enumerate(rows):
+        before = jnp.concatenate([load_rows(tile_ref, k, t, r) for t in range(tile_ref.shape[1])], axis=1)
+        store_rows(tile_ref, k, r, before - sums[j * planes : (j + 1) * planes])
+
+
 def first_kernel(
-    recv_ref, rhs_ref, perm_ref, r1_ref, edge_ref, pair_ref, other_ref, hi_ref, lo_ref, acc_ref, tile_ref
+    recv_ref, rhs_ref, perm_ref, kept_ref, edge_ref, pair_ref, other_ref, hi_ref, lo_ref, acc_ref, tile_ref
 ):
     split_cells(recv_ref, hi_ref, lo_ref)
-    incident, fields = scatter_slots(recv_ref, hi_ref, lo_ref, acc_ref, ((ALL, (3, 4), False), (EDGES,) + FIELDS))
+    incident, fields = scatter_slots(recv_ref, hi_ref, lo_ref, acc_ref, ((OUTER, (3, 4), False), (EDGES,) + FIELDS))
     planes = perm_ref.shape[0] // 8
     for k in range(2):
-        for r in range(8):
-            store_rows(tile_ref, k, r, incident[k][r * planes : (r + 1) * planes])
-    for k in range(2):
-        inc = jnp.concatenate([tile_ref[k, t] for t in range(tile_ref.shape[1])], axis=1)
-        value = rhs_ref[k] - inc
-        r1_ref[k] = value
-        keep_tiles(tile_ref, k, value)
+        keep_tiles(tile_ref, k, rhs_ref[k])
+        subtract_rows(tile_ref, k, OUTER, incident[k])
+        kept_ref[k] = tile_ref[k]
     keep_tiles(tile_ref, 2, perm_ref[...])
     fields = [TAU * fields[3]] + fields[:3]
     for k in range(4):
@@ -196,8 +200,12 @@
                 other_ref[rows, lanes] = jnp.where(even, first, last)
 
 
-def second_kernel(recv_ref, hi_ref, lo_ref, edge_ref, wn_ref, acc_ref):
-    (fields,) = scatter_slots(recv_ref, hi_ref, lo_ref, acc_ref, ((INNER,) + FIELDS,))
+def second_kernel(recv_ref, hi_ref, lo_ref, kept_ref, edge_ref, r1_ref, wn_ref, acc_ref, tile_ref):
+    incident, fields = scatter_slots(recv_ref, hi_ref, lo_ref, acc_ref, ((MIDDLE, (3, 4), False), (INNER,) + FIELDS))
+    for k in range(2):
+        tile_ref[k] = kept_ref[k]
+        subtract_rows(tile_ref, k, MIDDLE, incident[k])
+        r1_ref[k] = jnp.concatenate([tile_ref[k, t] for t in range(tile_ref.shape[1])], axis=1)
     planes = edge_ref.shape[1] // 2
     for k, value in enumerate([TAU * fields[3]] + fields[:3]):
         for j, r in enumerate(EDGES):
@@ -410,11 +418,11 @@
         return pl.CostEstimate(flops=flops, transcendentals=0, bytes_accessed=slots * CHANNELS * points * 4)
 
     strip = shape(13 * planes, cols)
-    parts = 4 * cells + 14 * planes
+    parts = 24 * planes + 14 * planes
     local = shape(slots, points)
-    r1, edges, pair, other, hi, lo = pl.pallas_call(
+    kept, edges, pair, other, hi, lo = pl.pallas_call(
         first_kernel,
-        out_shape=(shape(2, cells, cols), shape(4, 2 * planes, cols), strip, strip, local, local),
+        out_shape=(shape(2, tiles, cells, 128), shape(4, 2 * planes, cols), strip, strip, local, local),
         in_specs=in_vmem(3),
         out_specs=tuple(in_vmem(6)),
         scratch_shapes=[pltpu.VMEM((parts, cols), f32), pltpu.VMEM((3, tiles, cells, 128), f32)],
@@ -424,17 +432,17 @@
     )(recv, rhs_field, permittivity)
     from_other = lax.ppermute(other, "gx", [(i, (((i + 1) ^ 1) - 1) % gx) for i in range(gx)])
     from_pair = lax.ppermute(pair, "gx", [(i, i ^ 1) for i in range(gx)])
-    parts = 7 * 6 * planes
-    wn = pl.pallas_call(
+    parts = 7 * 6 * planes + 4 * 2 * planes
+    r1, wn = pl.pallas_call(
         second_kernel,
-        out_shape=shape(4, tiles, cells, 128),
-        in_specs=in_vmem(4),
-        out_specs=in_vmem(1)[0],
-        scratch_shapes=[pltpu.VMEM((parts, cols), f32)],
+        out_shape=(shape(2, cells, cols), shape(4, tiles, cells, 128)),
+        in_specs=in_vmem(5),
+        out_specs=tuple(in_vmem(2)),
+        scratch_shapes=[pltpu.VMEM((parts, cols), f32), pltpu.VMEM((2, tiles, cells, 128), f32)],
         compiler_params=params,
         cost_estimate=cost(parts),
         name="second",
-    )(recv, hi, lo, edges)
+    )(recv, hi, lo, kept, edges)
     pair, other, halo = pl.pallas_call(
         strip_kernel,
         out_shape=(shape(16, 128), shape(16, 128), shape(7, tiles, cells, 128)),

time: 53.2 us -> 52.2 us (0.981)
  starting transfers between devices: 6.56 us -> 5.66 us
    ppermute x1, starting transfers between devices: 2.51 us -> 1.44 us  [per_device(): lax.ppermute(other, 'gy', [(i, ((i + 1 ^ 1) - 1) % gy) for i in range(gy)])]
  transfers between devices with their start and end apart: 4 -> 4, of which waited for: 2 -> 2; matrix products, arithmetic and copies ran while one was open for 0% -> 0% of each run, Pallas kernels for 13% -> 15%
where the time goes in v6:
time: 52.2 us; the launch traced here: 52 us
  blocking collectives  27.4 us (52%)
  Pallas kernels  17.2 us (33%)
  starting transfers between devices  5.66 us (11%)
  waiting for transfers between devices  1 us (2%)
  between operations  0.71 us (1%)
    all_to_all x1, blocking collectives, per_device(): lax.all_to_all(send.reshape(-1), ('gx', 'gy'), split_axis=0, concat_axis=...  27.4 us
    pallas_call x1, Pallas kernels, per_device(): pl.pallas_call(second_kernel, out_shape=(shape(2, cells, cols), shape(4,...  7.26 us
    pallas_call x1, Pallas kernels, per_device(): pl.pallas_call(first_kernel, out_shape=(shape(2, tiles, cells, 128), shap...  5.67 us
    ppermute x1, starting transfers between devices, per_device(): lax.ppermute(other, 'gx', [(i, ((i + 1 ^ 1) - 1) % gx) for i in range(gx)])  3.08 us
    pallas_call x1, Pallas kernels, per_device(): pl.pallas_call(pack_kernel, out_shape=shape(slots * CHANNELS, points), in...  1.62 us
    pallas_call x1, Pallas kernels, per_device(): pl.pallas_call(final_kernel, out_shape=(field, field), in_specs=in_vmem(8...  1.56 us
    ppermute x1, starting transfers between devices, per_device(): lax.ppermute(other, 'gy', [(i, ((i + 1 ^ 1) - 1) % gy) for i in range(gy)])  1.44 us
  transfers between devices with their start and end apart: 4, of which 2 were waited for; matrix products, arithmetic and copies ran while one was open for 0% of the time, Pallas kernels for 15%

profile of v6, /device:TPU:1, one launch (start us, length us, event | category | flops | bytes accessed | tf_op | source)
XLA Modules:
  0.0 52.0 jit_solution(4685302492389392829)
XLA Ops:
  0.6 1.6 %pack.1 = f32[1536,128]{1,0:T(8,128)S(1)} custom-call(s32[128]{0:T(128)} %bitcast.13, f32[128,128]{1,0:T(8,128)} %dist_hbm.1, f32[3,128,128]{2,1,0:T(8,128)} %normal_hbm.1, f32[2,128,128]{2,1,0:T(8,128)} %inc_hbm.1, s32[128,128]{1,0:T(8,128)} %cell_hbm.1, s32[128,128]{1,0:T(8,128)} %mask_hbm.1), custom_call_target="tpu_custom_call" | custom-call | tf_op jit(solution)/shard_map/pack/pallas_call | solution.py:387
  2.3 0.0 copy-start
  2.3 0.0 copy-start.1
  2.3 27.4 %all_to_all.9 = f32[128,1536,1]{1,2,0:T(1,128)S(1)} all-to-all(f32[128,1536,1]{1,2,0:T(1,128)S(1)} %bitcast.5), channel_id=1, replica_groups=mesh['gx'=32,'gy'=4] {'gx','gy'}, dimensions={0} | all-to-all | bytes 1572864 | tf_op jit(solution)/shard_map/all_to_all | solution.py:408
  29.7 0.0 copy-done
  29.7 0.0 copy-done.1
  29.7 5.7 %first.1 = (f32[2,2,64,128]{3,2,1,0:T(8,128)S(1)}, f32[4,16,256]{2,1,0:T(8,128)S(1)}, f32[104,256]{1,0:T(8,128)S(1)}, f32[104,256]{1,0:T(8,128)S(1)}, f32[256,128]{1,0:T(8,128)S(1)}, /*index=5*/f32[256,128]{1,0:T(8,128)S(1)}) custom-call(f32[1536,128]{1,0:T(8,128)S(1)} %bitcast.6, f32[2,64,256]{2,1,0:T(8,128)S(1)} %bitcast.12, f32[64,256]{1,0:T(8,128)S(1)} %bitcast.8), custom_call_target="tpu_custom_call" | custom-call | flops 5100273664 | bytes 786432 | tf_op jit(solution)/shard_map/first/pallas_call | solution.py:423
  35.4 0.9 %collective-permute-start = (f32[104,256]{1,0:T(8,128)S(1)}, f32[104,256]{1,0:T(8,128)S(1)}, u32[]{:S(2)}, u32[]{:S(2)}) collective-permute-start(f32[104,256]{1,0:T(8,128)S(1)} %get-tuple-element.22), channel_id=1, source_target_pairs={{0,4},{4,0},{8,12},{12,8},{16,20},{20,16},{24,28},{28,24},{32,36},... | collective-permute-start | bytes 319496 | tf_op jit(solution)/shard_map/ppermute | solution.py:434
  36.3 3.1 %collective-permute-start.1 = (f32[104,256]{1,0:T(8,128)S(1)}, f32[104,256]{1,0:T(8,128)S(1)}, u32[]{:S(2)}, u32[]{:S(2)}) collective-permute-start(f32[104,256]{1,0:T(8,128)S(1)} %get-tuple-element.23), channel_id=1, source_target_pairs={{0,124},{4,8},{8,4},{12,16},{16,12},{20,24},{24,20},{28,32},{32,28... | collective-permute-start | bytes 319496 | tf_op jit(solution)/shard_map/ppermute | solution.py:433
  39.4 7.3 %second.1 = (f32[2,64,256]{2,1,0:T(8,128)S(1)}, f32[4,2,64,128]{3,2,1,0:T(8,128)S(1)}) custom-call(f32[1536,128]{1,0:T(8,128)S(1)} %bitcast.7, f32[256,128]{1,0:T(8,128)S(1)} %get-tuple-element.16.hi_ref, f32[256,128]{1,0:T(8,128)S(1)} %get-tuple-element.17.lo_ref, f32[2,2,64,128]{3,2,1,0:T(8,128)S(1)} %get-tuple-element.18.kept_ref, ...), custom_call_target="tpu_custom_call" | custom-call | flops 6710886400 | bytes 786432 | tf_op jit(solution)/shard_map/second/pallas_call | solution.py:436
  46.7 0.0 collective-permute-done.pair_ref
  46.7 0.0 collective-permute-done.1.other_ref
  46.7 0.3 strips.1
  47.0 1.4 %collective-permute-start.3 = (f32[16,128]{1,0:T(8,128)S(1)}, f32[16,128]{1,0:T(8,128)S(1)}, u32[]{:S(2)}, u32[]{:S(2)}) collective-permute-start(f32[16,128]{1,0:T(8,128)S(1)} %get-tuple-element.29), channel_id=1, source_target_pairs={{0,3},{1,2},{2,1},{3,0},{4,7},{5,6},{6,5},{7,4},{8,11},{9,10},{10,... | collective-permute-start | bytes 24584 | tf_op jit(solution)/shard_map/ppermute | solution.py:454
  48.4 0.7 %inner.1 = (f32[2,8,8,256]{3,2,1,0:T(8,128)S(1)}, f32[2,8,8,256]{3,2,1,0:T(8,128)S(1)}, f32[16,128]{1,0:T(8,128)S(1)}) custom-call(f32[2,64,256]{2,1,0:T(8,128)S(1)} %get-tuple-element.20.r1_ref, f32[64,256]{1,0:T(8,128)S(1)} %bitcast.10, f32[4,2,64,128]{3,2,1,0:T(8,128)S(1)} %get-tuple-element.21.wn_ref, f32[7,2,64,128]{3,2,1,0:T(8,128)S(1)} %get-tuple-element.24.halo_ref, ...), custom_call_target="tpu_custom_call" | custom-call | flops 1073741824 | bytes 786432 | tf_op jit(solution)/shard_map/inner/pallas_call | solution.py:456
  49.2 0.3 collective-permute-start.2
  49.5 0.7 %collective-permute-done.3.other_ref = f32[16,128]{1,0:T(8,128)S(1)} collective-permute-done((f32[16,128]{1,0:T(8,128)S(1)}, f32[16,128]{1,0:T(8,128)S(1)}, u32[]{:S(2)}, u32[]{:S(2)}) %collective-permute-start.3) | collective-permute-done | bytes 8224 | tf_op jit(solution)/shard_map/ppermute | solution.py:454
  50.2 0.3 collective-permute-done.2.pair_ref
  50.5 1.6 %final.1 = (f32[2,8,8,256]{3,2,1,0:T(8,128)}, f32[2,8,8,256]{3,2,1,0:T(8,128)}) custom-call(f32[2,64,256]{2,1,0:T(8,128)S(1)} %get-tuple-element.20.r1_ref, f32[64,256]{1,0:T(8,128)S(1)} %bitcast.11, f32[4,2,64,128]{3,2,1,0:T(8,128)S(1)} %get-tuple-element.21.wn_ref, f32[7,2,64,128]{3,2,1,0:T(8,128)S(1)} %get-tuple-element.24.halo_ref, ...), custom_call_target="tpu_custom_call" | custom-call | tf_op jit(solution)/shard_map/final/pallas_call | solution.py:466
Async XLA Ops:
  2.3 27.5 %copy-start = (f32[8,8,256]{2,1,0:T(8,128)S(1)}, f32[8,8,256]{2,1,0:T(8,128)}, u32[]{:S(2)}) copy-start(f32[8,8,256]{2,1,0:T(8,128)} %param.9) | copy-start | bytes 196612
  2.3 27.5 %copy-start.1 = (f32[2,8,8,256]{3,2,1,0:T(8,128)S(1)}, f32[2,8,8,256]{3,2,1,0:T(8,128)}, u32[]{:S(2)}) copy-start(f32[2,8,8,256]{3,2,1,0:T(8,128)} %param.8) | copy-start | bytes 393220
  35.4 11.2 %collective-permute-start = (f32[104,256]{1,0:T(8,128)S(1)}, f32[104,256]{1,0:T(8,128)S(1)}, u32[]{:S(2)}, u32[]{:S(2)}) collective-permute-start(f32[104,256]{1,0:T(8,128)S(1)} %get-tuple-element.22), channel_id=1, source_target_pairs={{0,4},{4,0},{8,12},{12,8},{16,20},{20,16},{24,28},{28,24},{32,36},... | collective-permute-start | bytes 319496 | tf_op jit(solution)/shard_map/ppermute | solution.py:434
  36.3 10.4 %collective-permute-start.1 = (f32[104,256]{1,0:T(8,128)S(1)}, f32[104,256]{1,0:T(8,128)S(1)}, u32[]{:S(2)}, u32[]{:S(2)}) collective-permute-start(f32[104,256]{1,0:T(8,128)S(1)} %get-tuple-element.23), channel_id=1, source_target_pairs={{0,124},{4,8},{8,4},{12,16},{16,12},{20,24},{24,20},{28,32},{32,28... | collective-permute-start | bytes 319496 | tf_op jit(solution)/shard_map/ppermute | solution.py:433
  47.0 3.2 %collective-permute-start.3 = (f32[16,128]{1,0:T(8,128)S(1)}, f32[16,128]{1,0:T(8,128)S(1)}, u32[]{:S(2)}, u32[]{:S(2)}) collective-permute-start(f32[16,128]{1,0:T(8,128)S(1)} %get-tuple-element.29), channel_id=1, source_target_pairs={{0,3},{1,2},{2,1},{3,0},{4,7},{5,6},{6,5},{7,4},{8,11},{9,10},{10,... | collective-permute-start | bytes 24584 | tf_op jit(solution)/shard_map/ppermute | solution.py:454
  49.2 1.3 %collective-permute-start.2 = (f32[16,128]{1,0:T(8,128)S(1)}, f32[16,128]{1,0:T(8,128)S(1)}, u32[]{:S(2)}, u32[]{:S(2)}) collective-permute-start(f32[16,128]{1,0:T(8,128)S(1)} %get-tuple-element.28), channel_id=1, source_target_pairs={{0,1},{1,0},{2,3},{3,2},{4,5},{5,4},{6,7},{7,6},{8,9},{9,8},{10,11... | collective-permute-start | bytes 24584 | tf_op jit(solution)/shard_map/ppermute | solution.py:465

commit v7 on v6

--- a/solution.py
+++ b/solution.py
@@ -333,11 +333,18 @@
         res_ref[k] = res[:, 0:8, :]
 
 
-def final_kernel(
-    r1_ref, perm_ref, wn_ref, halo_ref, sol_in_ref, res_in_ref, pair_ref, other_ref, sol_ref, res_ref
-):
-    planes = perm_ref.shape[0] // 8
+def near_kernel(r1_ref, perm_ref, wn_ref, halo_ref, near_ref):
+    lane = lax.broadcasted_iota(jnp.int32, near_ref.shape[1:], 2)
     last = halo_ref.shape[1] - 1
+    for c in range(7):
+        head = tile_of(c, 0, r1_ref, perm_ref, wn_ref, halo_ref)
+        tail = pltpu.roll(tile_of(c, last, r1_ref, perm_ref, wn_ref, halo_ref), 116, axis=2)
+        near_ref[c] = jnp.where(lane < 56, head, jnp.where((lane >= 60) & (lane < 116), tail, 0.0))
+
+
+def final_kernel(near_ref, sol_in_ref, res_in_ref, pair_ref, other_ref, sol_ref, res_ref):
+    planes = near_ref.shape[1]
+    last = sol_ref.shape[3] // 128 - 1
     lane = lax.broadcasted_iota(jnp.int32, (planes, 16, 128), 2)
     even = lax.rem(lax.axis_index("gy"), 2) == 0
     pair, other = pair_ref[...], other_ref[...]
@@ -348,10 +355,8 @@
     fields = []
     for c in range(7):
         offset, width = COL_PLACE[c]
-        args = (r1_ref, perm_ref, wn_ref, halo_ref)
-        field = jnp.where(lane < 56, tile_of(c, 0, *args), 0.0)
-        field = jnp.where((lane >= 60) & (lane < 116), pltpu.roll(tile_of(c, last, *args), 116, axis=2), field)
-        field = jnp.where((lane >= 116) & (lane < 116 + width), pltpu.roll(from_right, 116 - offset, axis=2), field)
+        right = (lane >= 116) & (lane < 116 + width)
+        field = jnp.where(right, pltpu.roll(from_right, 116 - offset, axis=2), near_ref[c])
         field = jnp.where(lane >= 128 - width, pltpu.roll(from_left, offset, axis=2), field)
         fields.append(field)
     sa, sb, ra, rb = iterate(*fields)
@@ -462,15 +467,24 @@
         cost_estimate=cost(8 * planes),
         name="inner",
     )(r1, permittivity, wn, halo, pair)
+    near = pl.pallas_call(
+        near_kernel,
+        out_shape=shape(7, planes, 16, 128),
+        in_specs=in_vmem(4),
+        out_specs=in_vmem(1)[0],
+        compiler_params=params,
+        cost_estimate=cost(8 * planes),
+        name="near",
+    )(r1, permittivity, wn, halo)
     from_pair = lax.ppermute(pair, "gy", [(i, i ^ 1) for i in range(gy)])
     return pl.pallas_call(
         final_kernel,
         out_shape=(field, field),
-        in_specs=in_vmem(8),
+        in_specs=in_vmem(5),
         out_specs=tuple(in_vmem(2)),
         compiler_params=params,
         name="final",
-    )(r1, permittivity, wn, halo, sol, res, from_pair, from_other)
+    )(near, sol, res, from_pair, from_other)
 
 
 def solution(mesh):

time: 52.2 us -> 52.1 us (level)
    pallas_call x1 -> x2, Pallas kernels: 1.56 us -> 1.65 us  [the longest x1 1.46 us: per_device(): pl.pallas_call(final_kernel, out_shape=(field, field), in_specs=in_vmem(5...]
  transfers between devices with their start and end apart: 4 -> 4, of which waited for: 2 -> 2; matrix products, arithmetic and copies ran while one was open for 0% -> 0% of each run, Pallas kernels for 15% -> 16%
where the time goes in v7:
time: 52.1 us; the launch traced here: 51.9 us
  blocking collectives  27.4 us (53%)
  Pallas kernels  17.3 us (33%)
  starting transfers between devices  5.66 us (11%)
  waiting for transfers between devices  0.81 us (2%)
  between operations  0.71 us (1%)
    all_to_all x1, blocking collectives, per_device(): lax.all_to_all(send.reshape(-1), ('gx', 'gy'), split_axis=0, concat_axis=...  27.4 us
    pallas_call x1, Pallas kernels, per_device(): pl.pallas_call(second_kernel, out_shape=(shape(2, cells, cols), shape(4,...  7.26 us
    pallas_call x1, Pallas kernels, per_device(): pl.pallas_call(first_kernel, out_shape=(shape(2, tiles, cells, 128), shap...  5.67 us
    ppermute x1, starting transfers between devices, per_device(): lax.ppermute(other, 'gx', [(i, ((i + 1 ^ 1) - 1) % gx) for i in range(gx)])  3.08 us
    pallas_call x1, Pallas kernels, per_device(): pl.pallas_call(pack_kernel, out_shape=shape(slots * CHANNELS, points), in...  1.62 us
    pallas_call x1, Pallas kernels, per_device(): pl.pallas_call(final_kernel, out_shape=(field, field), in_specs=in_vmem(5...  1.46 us
    ppermute x1, starting transfers between devices, per_device(): lax.ppermute(other, 'gy', [(i, ((i + 1 ^ 1) - 1) % gy) for i in range(gy)])  1.44 us
  transfers between devices with their start and end apart: 4, of which 2 were waited for; matrix products, arithmetic and copies ran while one was open for 0% of the time, Pallas kernels for 16%

profile of v7, /device:TPU:1, one launch (start us, length us, event | category | flops | bytes accessed | tf_op | source)
XLA Modules:
  0.0 51.9 jit_solution(16484771270455163125)
XLA Ops:
  0.6 1.6 %pack.1 = f32[1536,128]{1,0:T(8,128)S(1)} custom-call(s32[128]{0:T(128)} %bitcast.13, f32[128,128]{1,0:T(8,128)} %dist_hbm.1, f32[3,128,128]{2,1,0:T(8,128)} %normal_hbm.1, f32[2,128,128]{2,1,0:T(8,128)} %inc_hbm.1, s32[128,128]{1,0:T(8,128)} %cell_hbm.1, s32[128,128]{1,0:T(8,128)} %mask_hbm.1), custom_call_target="tpu_custom_call" | custom-call | tf_op jit(solution)/shard_map/pack/pallas_call | solution.py:392
  2.3 0.0 copy-start
  2.3 0.0 copy-start.1
  2.3 27.4 %all_to_all.9 = f32[128,1536,1]{1,2,0:T(1,128)S(1)} all-to-all(f32[128,1536,1]{1,2,0:T(1,128)S(1)} %bitcast.5), channel_id=1, replica_groups=mesh['gx'=32,'gy'=4] {'gx','gy'}, dimensions={0} | all-to-all | bytes 1572864 | tf_op jit(solution)/shard_map/all_to_all | solution.py:413
  29.7 0.0 copy-done
  29.7 0.0 copy-done.1
  29.7 5.7 %first.1 = (f32[2,2,64,128]{3,2,1,0:T(8,128)S(1)}, f32[4,16,256]{2,1,0:T(8,128)S(1)}, f32[104,256]{1,0:T(8,128)S(1)}, f32[104,256]{1,0:T(8,128)S(1)}, f32[256,128]{1,0:T(8,128)S(1)}, /*index=5*/f32[256,128]{1,0:T(8,128)S(1)}) custom-call(f32[1536,128]{1,0:T(8,128)S(1)} %bitcast.6, f32[2,64,256]{2,1,0:T(8,128)S(1)} %bitcast.12, f32[64,256]{1,0:T(8,128)S(1)} %bitcast.8), custom_call_target="tpu_custom_call" | custom-call | flops 5100273664 | bytes 786432 | tf_op jit(solution)/shard_map/first/pallas_call | solution.py:428
  35.4 0.9 %collective-permute-start = (f32[104,256]{1,0:T(8,128)S(1)}, f32[104,256]{1,0:T(8,128)S(1)}, u32[]{:S(2)}, u32[]{:S(2)}) collective-permute-start(f32[104,256]{1,0:T(8,128)S(1)} %get-tuple-element.22), channel_id=1, source_target_pairs={{0,4},{4,0},{8,12},{12,8},{16,20},{20,16},{24,28},{28,24},{32,36},... | collective-permute-start | bytes 319496 | tf_op jit(solution)/shard_map/ppermute | solution.py:439
  36.3 3.1 %collective-permute-start.1 = (f32[104,256]{1,0:T(8,128)S(1)}, f32[104,256]{1,0:T(8,128)S(1)}, u32[]{:S(2)}, u32[]{:S(2)}) collective-permute-start(f32[104,256]{1,0:T(8,128)S(1)} %get-tuple-element.23), channel_id=1, source_target_pairs={{0,124},{4,8},{8,4},{12,16},{16,12},{20,24},{24,20},{28,32},{32,28... | collective-permute-start | bytes 319496 | tf_op jit(solution)/shard_map/ppermute | solution.py:438
  39.4 7.3 %second.1 = (f32[2,64,256]{2,1,0:T(8,128)S(1)}, f32[4,2,64,128]{3,2,1,0:T(8,128)S(1)}) custom-call(f32[1536,128]{1,0:T(8,128)S(1)} %bitcast.7, f32[256,128]{1,0:T(8,128)S(1)} %get-tuple-element.16.hi_ref, f32[256,128]{1,0:T(8,128)S(1)} %get-tuple-element.17.lo_ref, f32[2,2,64,128]{3,2,1,0:T(8,128)S(1)} %get-tuple-element.18.kept_ref, ...), custom_call_target="tpu_custom_call" | custom-call | flops 6710886400 | bytes 786432 | tf_op jit(solution)/shard_map/second/pallas_call | solution.py:441
  46.7 0.0 collective-permute-done.pair_ref
  46.7 0.0 collective-permute-done.1.other_ref
  46.7 0.3 strips.1
  47.0 1.4 %collective-permute-start.3 = (f32[16,128]{1,0:T(8,128)S(1)}, f32[16,128]{1,0:T(8,128)S(1)}, u32[]{:S(2)}, u32[]{:S(2)}) collective-permute-start(f32[16,128]{1,0:T(8,128)S(1)} %get-tuple-element.29), channel_id=1, source_target_pairs={{0,3},{1,2},{2,1},{3,0},{4,7},{5,6},{6,5},{7,4},{8,11},{9,10},{10,... | collective-permute-start | bytes 24584 | tf_op jit(solution)/shard_map/ppermute | solution.py:459
  48.4 0.7 %inner.1 = (f32[2,8,8,256]{3,2,1,0:T(8,128)S(1)}, f32[2,8,8,256]{3,2,1,0:T(8,128)S(1)}, f32[16,128]{1,0:T(8,128)S(1)}) custom-call(f32[2,64,256]{2,1,0:T(8,128)S(1)} %get-tuple-element.20.r1_ref, f32[64,256]{1,0:T(8,128)S(1)} %bitcast.10, f32[4,2,64,128]{3,2,1,0:T(8,128)S(1)} %get-tuple-element.21.wn_ref, f32[7,2,64,128]{3,2,1,0:T(8,128)S(1)} %get-tuple-element.24.halo_ref, ...), custom_call_target="tpu_custom_call" | custom-call | flops 1073741824 | bytes 786432 | tf_op jit(solution)/shard_map/inner/pallas_call | solution.py:461
  49.2 0.3 collective-permute-start.2
  49.5 0.2 near.1.near_ref
  49.6 0.5 collective-permute-done.3.other_ref
  50.2 0.3 collective-permute-done.2.pair_ref
  50.4 1.5 %final.1 = (f32[2,8,8,256]{3,2,1,0:T(8,128)}, f32[2,8,8,256]{3,2,1,0:T(8,128)}) custom-call(f32[7,8,16,128]{3,2,1,0:T(8,128)S(1)} %near.1.near_ref, f32[2,8,8,256]{3,2,1,0:T(8,128)S(1)} %get-tuple-element.26.sol_in_ref, f32[2,8,8,256]{3,2,1,0:T(8,128)S(1)} %get-tuple-element.27.res_in_ref, f32[16,128]{1,0:T(8,128)S(1)} %collective-permute-done.2.pair_ref, ...), custom_call_target="tpu_custom_call" | custom-call | tf_op jit(solution)/shard_map/final/pallas_call | solution.py:480
Async XLA Ops:
  2.3 27.5 %copy-start = (f32[8,8,256]{2,1,0:T(8,128)S(1)}, f32[8,8,256]{2,1,0:T(8,128)}, u32[]{:S(2)}) copy-start(f32[8,8,256]{2,1,0:T(8,128)} %param.9) | copy-start | bytes 196612
  2.3 27.5 %copy-start.1 = (f32[2,8,8,256]{3,2,1,0:T(8,128)S(1)}, f32[2,8,8,256]{3,2,1,0:T(8,128)}, u32[]{:S(2)}) copy-start(f32[2,8,8,256]{3,2,1,0:T(8,128)} %param.8) | copy-start | bytes 393220
  35.4 11.2 %collective-permute-start = (f32[104,256]{1,0:T(8,128)S(1)}, f32[104,256]{1,0:T(8,128)S(1)}, u32[]{:S(2)}, u32[]{:S(2)}) collective-permute-start(f32[104,256]{1,0:T(8,128)S(1)} %get-tuple-element.22), channel_id=1, source_target_pairs={{0,4},{4,0},{8,12},{12,8},{16,20},{20,16},{24,28},{28,24},{32,36},... | collective-permute-start | bytes 319496 | tf_op jit(solution)/shard_map/ppermute | solution.py:439
  36.3 10.4 %collective-permute-start.1 = (f32[104,256]{1,0:T(8,128)S(1)}, f32[104,256]{1,0:T(8,128)S(1)}, u32[]{:S(2)}, u32[]{:S(2)}) collective-permute-start(f32[104,256]{1,0:T(8,128)S(1)} %get-tuple-element.23), channel_id=1, source_target_pairs={{0,124},{4,8},{8,4},{12,16},{16,12},{20,24},{24,20},{28,32},{32,28... | collective-permute-start | bytes 319496 | tf_op jit(solution)/shard_map/ppermute | solution.py:438
  47.0 3.2 %collective-permute-start.3 = (f32[16,128]{1,0:T(8,128)S(1)}, f32[16,128]{1,0:T(8,128)S(1)}, u32[]{:S(2)}, u32[]{:S(2)}) collective-permute-start(f32[16,128]{1,0:T(8,128)S(1)} %get-tuple-element.29), channel_id=1, source_target_pairs={{0,3},{1,2},{2,1},{3,0},{4,7},{5,6},{6,5},{7,4},{8,11},{9,10},{10,... | collective-permute-start | bytes 24584 | tf_op jit(solution)/shard_map/ppermute | solution.py:459
  49.2 1.3 %collective-permute-start.2 = (f32[16,128]{1,0:T(8,128)S(1)}, f32[16,128]{1,0:T(8,128)S(1)}, u32[]{:S(2)}, u32[]{:S(2)}) collective-permute-start(f32[16,128]{1,0:T(8,128)S(1)} %get-tuple-element.28), channel_id=1, source_target_pairs={{0,1},{1,0},{2,3},{3,2},{4,5},{5,4},{6,7},{7,6},{8,9},{9,8},{10,11... | collective-permute-start | bytes 24584 | tf_op jit(solution)/shard_map/ppermute | solution.py:479

commit v8 on v7

--- a/solution.py
+++ b/solution.py
@@ -61,7 +61,7 @@
         out_ref[pl.ds(base, CHANNELS), :] = coef_ref[pl.ds(b, CHANNELS, stride=blocks), :]
         return carry
 
-    lax.fori_loop(0, blocks, place, 0, unroll=8)
+    lax.fori_loop(0, blocks, place, 0, unroll=4)
 
 
 def split_cells(recv_ref, hi_ref, lo_ref):

time: 52.1 us -> 52.2 us (level)
  no operation moved by 1% of the time
where the time goes in v8:
time: 52.2 us; the launch traced here: 52 us
  blocking collectives  27.4 us (52%)
  Pallas kernels  17.4 us (33%)
  starting transfers between devices  5.66 us (11%)
  waiting for transfers between devices  0.81 us (2%)
  between operations  0.71 us (1%)
    all_to_all x1, blocking collectives, per_device(): lax.all_to_all(send.reshape(-1), ('gx', 'gy'), split_axis=0, concat_axis=...  27.4 us
    pallas_call x1, Pallas kernels, per_device(): pl.pallas_call(second_kernel, out_shape=(shape(2, cells, cols), shape(4,...  7.26 us
    pallas_call x1, Pallas kernels, per_device(): pl.pallas_call(first_kernel, out_shape=(shape(2, tiles, cells, 128), shap...  5.67 us
    ppermute x1, starting transfers between devices, per_device(): lax.ppermute(other, 'gx', [(i, ((i + 1 ^ 1) - 1) % gx) for i in range(gx)])  3.08 us
    pallas_call x1, Pallas kernels, per_device(): pl.pallas_call(pack_kernel, out_shape=shape(slots * CHANNELS, points), in...  1.75 us
    pallas_call x1, Pallas kernels, per_device(): pl.pallas_call(final_kernel, out_shape=(field, field), in_specs=in_vmem(5...  1.46 us
    ppermute x1, starting transfers between devices, per_device(): lax.ppermute(other, 'gy', [(i, ((i + 1 ^ 1) - 1) % gy) for i in range(gy)])  1.44 us
  transfers between devices with their start and end apart: 4, of which 2 were waited for; matrix products, arithmetic and copies ran while one was open for 0% of the time, Pallas kernels for 16%

profile of v8, /device:TPU:1, one launch (start us, length us, event | category | flops | bytes accessed | tf_op | source)
XLA Modules:
  0.0 52.0 jit_solution(13748548013373315126)
XLA Ops:
  0.6 1.7 %pack.1 = f32[1536,128]{1,0:T(8,128)S(1)} custom-call(s32[128]{0:T(128)} %bitcast.13, f32[128,128]{1,0:T(8,128)} %dist_hbm.1, f32[3,128,128]{2,1,0:T(8,128)} %normal_hbm.1, f32[2,128,128]{2,1,0:T(8,128)} %inc_hbm.1, s32[128,128]{1,0:T(8,128)} %cell_hbm.1, s32[128,128]{1,0:T(8,128)} %mask_hbm.1), custom_call_target="tpu_custom_call" | custom-call | tf_op jit(solution)/shard_map/pack/pallas_call | solution.py:392
  2.4 0.0 copy-start
  2.4 0.0 copy-start.1
  2.4 27.4 %all_to_all.9 = f32[128,1536,1]{1,2,0:T(1,128)S(1)} all-to-all(f32[128,1536,1]{1,2,0:T(1,128)S(1)} %bitcast.5), channel_id=1, replica_groups=mesh['gx'=32,'gy'=4] {'gx','gy'}, dimensions={0} | all-to-all | bytes 1572864 | tf_op jit(solution)/shard_map/all_to_all | solution.py:413
  29.9 0.0 copy-done
  29.9 0.0 copy-done.1
  29.9 5.7 %first.1 = (f32[2,2,64,128]{3,2,1,0:T(8,128)S(1)}, f32[4,16,256]{2,1,0:T(8,128)S(1)}, f32[104,256]{1,0:T(8,128)S(1)}, f32[104,256]{1,0:T(8,128)S(1)}, f32[256,128]{1,0:T(8,128)S(1)}, /*index=5*/f32[256,128]{1,0:T(8,128)S(1)}) custom-call(f32[1536,128]{1,0:T(8,128)S(1)} %bitcast.6, f32[2,64,256]{2,1,0:T(8,128)S(1)} %bitcast.12, f32[64,256]{1,0:T(8,128)S(1)} %bitcast.8), custom_call_target="tpu_custom_call" | custom-call | flops 5100273664 | bytes 786432 | tf_op jit(solution)/shard_map/first/pallas_call | solution.py:428
  35.5 0.9 %collective-permute-start = (f32[104,256]{1,0:T(8,128)S(1)}, f32[104,256]{1,0:T(8,128)S(1)}, u32[]{:S(2)}, u32[]{:S(2)}) collective-permute-start(f32[104,256]{1,0:T(8,128)S(1)} %get-tuple-element.22), channel_id=1, source_target_pairs={{0,4},{4,0},{8,12},{12,8},{16,20},{20,16},{24,28},{28,24},{32,36},... | collective-permute-start | bytes 319496 | tf_op jit(solution)/shard_map/ppermute | solution.py:439
  36.4 3.1 %collective-permute-start.1 = (f32[104,256]{1,0:T(8,128)S(1)}, f32[104,256]{1,0:T(8,128)S(1)}, u32[]{:S(2)}, u32[]{:S(2)}) collective-permute-start(f32[104,256]{1,0:T(8,128)S(1)} %get-tuple-element.23), channel_id=1, source_target_pairs={{0,124},{4,8},{8,4},{12,16},{16,12},{20,24},{24,20},{28,32},{32,28... | collective-permute-start | bytes 319496 | tf_op jit(solution)/shard_map/ppermute | solution.py:438
  39.5 7.3 %second.1 = (f32[2,64,256]{2,1,0:T(8,128)S(1)}, f32[4,2,64,128]{3,2,1,0:T(8,128)S(1)}) custom-call(f32[1536,128]{1,0:T(8,128)S(1)} %bitcast.7, f32[256,128]{1,0:T(8,128)S(1)} %get-tuple-element.16.hi_ref, f32[256,128]{1,0:T(8,128)S(1)} %get-tuple-element.17.lo_ref, f32[2,2,64,128]{3,2,1,0:T(8,128)S(1)} %get-tuple-element.18.kept_ref, ...), custom_call_target="tpu_custom_call" | custom-call | flops 6710886400 | bytes 786432 | tf_op jit(solution)/shard_map/second/pallas_call | solution.py:441
  46.8 0.0 collective-permute-done.pair_ref
  46.8 0.0 collective-permute-done.1.other_ref
  46.8 0.3 strips.1
  47.1 1.4 %collective-permute-start.3 = (f32[16,128]{1,0:T(8,128)S(1)}, f32[16,128]{1,0:T(8,128)S(1)}, u32[]{:S(2)}, u32[]{:S(2)}) collective-permute-start(f32[16,128]{1,0:T(8,128)S(1)} %get-tuple-element.29), channel_id=1, source_target_pairs={{0,3},{1,2},{2,1},{3,0},{4,7},{5,6},{6,5},{7,4},{8,11},{9,10},{10,... | collective-permute-start | bytes 24584 | tf_op jit(solution)/shard_map/ppermute | solution.py:459
  48.6 0.7 %inner.1 = (f32[2,8,8,256]{3,2,1,0:T(8,128)S(1)}, f32[2,8,8,256]{3,2,1,0:T(8,128)S(1)}, f32[16,128]{1,0:T(8,128)S(1)}) custom-call(f32[2,64,256]{2,1,0:T(8,128)S(1)} %get-tuple-element.20.r1_ref, f32[64,256]{1,0:T(8,128)S(1)} %bitcast.10, f32[4,2,64,128]{3,2,1,0:T(8,128)S(1)} %get-tuple-element.21.wn_ref, f32[7,2,64,128]{3,2,1,0:T(8,128)S(1)} %get-tuple-element.24.halo_ref, ...), custom_call_target="tpu_custom_call" | custom-call | flops 1073741824 | bytes 786432 | tf_op jit(solution)/shard_map/inner/pallas_call | solution.py:461
  49.3 0.3 collective-permute-start.2
  49.6 0.2 near.1.near_ref
  49.8 0.5 collective-permute-done.3.other_ref
  50.3 0.3 collective-permute-done.2.pair_ref
  50.6 1.5 %final.1 = (f32[2,8,8,256]{3,2,1,0:T(8,128)}, f32[2,8,8,256]{3,2,1,0:T(8,128)}) custom-call(f32[7,8,16,128]{3,2,1,0:T(8,128)S(1)} %near.1.near_ref, f32[2,8,8,256]{3,2,1,0:T(8,128)S(1)} %get-tuple-element.26.sol_in_ref, f32[2,8,8,256]{3,2,1,0:T(8,128)S(1)} %get-tuple-element.27.res_in_ref, f32[16,128]{1,0:T(8,128)S(1)} %collective-permute-done.2.pair_ref, ...), custom_call_target="tpu_custom_call" | custom-call | tf_op jit(solution)/shard_map/final/pallas_call | solution.py:480
Async XLA Ops:
  2.4 27.5 %copy-start = (f32[8,8,256]{2,1,0:T(8,128)S(1)}, f32[8,8,256]{2,1,0:T(8,128)}, u32[]{:S(2)}) copy-start(f32[8,8,256]{2,1,0:T(8,128)} %param.9) | copy-start | bytes 196612
  2.4 27.5 %copy-start.1 = (f32[2,8,8,256]{3,2,1,0:T(8,128)S(1)}, f32[2,8,8,256]{3,2,1,0:T(8,128)}, u32[]{:S(2)}) copy-start(f32[2,8,8,256]{3,2,1,0:T(8,128)} %param.8) | copy-start | bytes 393220
  35.5 11.2 %collective-permute-start = (f32[104,256]{1,0:T(8,128)S(1)}, f32[104,256]{1,0:T(8,128)S(1)}, u32[]{:S(2)}, u32[]{:S(2)}) collective-permute-start(f32[104,256]{1,0:T(8,128)S(1)} %get-tuple-element.22), channel_id=1, source_target_pairs={{0,4},{4,0},{8,12},{12,8},{16,20},{20,16},{24,28},{28,24},{32,36},... | collective-permute-start | bytes 319496 | tf_op jit(solution)/shard_map/ppermute | solution.py:439
  36.4 10.4 %collective-permute-start.1 = (f32[104,256]{1,0:T(8,128)S(1)}, f32[104,256]{1,0:T(8,128)S(1)}, u32[]{:S(2)}, u32[]{:S(2)}) collective-permute-start(f32[104,256]{1,0:T(8,128)S(1)} %get-tuple-element.23), channel_id=1, source_target_pairs={{0,124},{4,8},{8,4},{12,16},{16,12},{20,24},{24,20},{28,32},{32,28... | collective-permute-start | bytes 319496 | tf_op jit(solution)/shard_map/ppermute | solution.py:438
  47.1 3.2 %collective-permute-start.3 = (f32[16,128]{1,0:T(8,128)S(1)}, f32[16,128]{1,0:T(8,128)S(1)}, u32[]{:S(2)}, u32[]{:S(2)}) collective-permute-start(f32[16,128]{1,0:T(8,128)S(1)} %get-tuple-element.29), channel_id=1, source_target_pairs={{0,3},{1,2},{2,1},{3,0},{4,7},{5,6},{6,5},{7,4},{8,11},{9,10},{10,... | collective-permute-start | bytes 24584 | tf_op jit(solution)/shard_map/ppermute | solution.py:459
  49.3 1.3 %collective-permute-start.2 = (f32[16,128]{1,0:T(8,128)S(1)}, f32[16,128]{1,0:T(8,128)S(1)}, u32[]{:S(2)}, u32[]{:S(2)}) collective-permute-start(f32[16,128]{1,0:T(8,128)S(1)} %get-tuple-element.28), channel_id=1, source_target_pairs={{0,1},{1,0},{2,3},{3,2},{4,5},{5,4},{6,7},{7,6},{8,9},{9,8},{10,11... | collective-permute-start | bytes 24584 | tf_op jit(solution)/shard_map/ppermute | solution.py:479
